TPU v7x, 512 devices: a whole 4x4x16 slice. The times are simulated.
512 devices in a mesh: ka: 16 (over z_hi, x), kp: 32 (over z_lo, y, core).
Axes of the slice: x: 4, y: 4, z: 16 (z_hi: 4, z_lo: 4; z = z_hi * 4 + z_lo), core: 2. Of those that a mesh axis runs over, the one named last changes fastest.
Arguments:
- waves: bfloat16 [32, 16, 4096], P('ka', None, 'kp'), may hold values from -6 to 6
- screen: float32 [32, 512], replicated, may hold values from 0.1 to 2
- pair_table: int32 [32, 32], P('ka', 'kp'), may hold values from 0 to 31
- plane_map: int32 [512], replicated, may hold values from 1 to 4095, as said below
- trial: bfloat16 [32, 64, 128], P('kp', None, 'ka'), may hold values from -6 to 6
- probe: bfloat16 [32, 64, 128], P('ka', None, 'kp'), may hold values from -6 to 6
Outputs:
- applied: float32 [32, 64, 128], P('ka', None, 'kp')
- adjoint: float32 [32, 64, 128], P('kp', None, 'ka')
Inputs may be any that keep to these rules, and one draw needn't show every extreme that they name: `plane_map`: the 512 values are distinct and none is 0.
All inputs are finite; a program needn't handle non-finite values.
Results may differ from a plain program's by a relative error of at most 0.0003.
Values may be sent and summed in bfloat16 or wider, within the bound.
No kernel may reach another device: no remote copies, remote signals or barrier semaphores. Data moves between devices by JAX's collectives and lax.ppermute only.
A program may use at most 64 MiB of HBM per device.

v0:
```python
import math

import jax
import jax.numpy as jnp
from jax import lax
from jax.sharding import PartitionSpec as P

NV = 8
NC = 8


def from_everyone(x, axis):
    count = lax.axis_size(axis)
    return lax.all_to_all(jnp.broadcast_to(x[None], (count, *x.shape)), axis, 0, 0, tiled=True)


def laid_out(tiles, dim):
    tiles = jnp.moveaxis(tiles, 0, dim)
    lengths = tiles.shape
    return tiles.reshape(*lengths[:dim], lengths[dim] * lengths[dim + 1], *lengths[dim + 2 :])


def collect(x, axis, dim):
    tiles = from_everyone(x, axis)
    return laid_out(tiles, dim)


def in_blocks(x, dim, count):
    lengths = x.shape
    tiles = x.reshape(*lengths[:dim], count, lengths[dim] // count, *lengths[dim + 1 :])
    return jnp.moveaxis(tiles, dim, 0)


def summed_on_arrival(x, axis, dim):
    tiles = in_blocks(x, dim, lax.axis_size(axis))
    arrived = lax.all_to_all(tiles, axis, split_axis=0, concat_axis=0, tiled=True)
    return arrived.sum(axis=0)


def make_tables(outer, inner):
    total = outer * inner
    first = jnp.arange(outer, dtype=jnp.int32)
    second = jnp.arange(inner, dtype=jnp.int32)
    phase_one = (first[:, None] * first[None, :] % outer).astype(jnp.float32) * (
        2.0 * math.pi / outer
    )
    phase_twist = (first[:, None] * second[None, :] % total).astype(jnp.float32) * (
        2.0 * math.pi / total
    )
    phase_two = (second[:, None] * second[None, :] % inner).astype(jnp.float32) * (
        2.0 * math.pi / inner
    )
    return (
        jnp.cos(phase_one),
        jnp.sin(phase_one),
        jnp.cos(phase_twist),
        jnp.sin(phase_twist),
        jnp.cos(phase_two),
        jnp.sin(phase_two),
    )


def spectrum(density, tables, chosen, outer, inner):
    cos_one, sin_one, cos_twist, sin_twist, cos_two, sin_two = tables
    high = lax.Precision.HIGHEST
    count = density.shape[0]
    grid = density.reshape(count, outer, inner)
    section_re = jnp.einsum("ga,nab->ngb", cos_one, grid, precision=high)
    section_im = -jnp.einsum("ga,nab->ngb", sin_one, grid, precision=high)
    twist_re = section_re * cos_twist + section_im * sin_twist
    twist_im = section_im * cos_twist - section_re * sin_twist
    final_re = jnp.einsum("ngb,bh->ngh", twist_re, cos_two, precision=high) + jnp.einsum(
        "ngb,bh->ngh", twist_im, sin_two, precision=high
    )
    final_im = jnp.einsum("ngb,bh->ngh", twist_im, cos_two, precision=high) - jnp.einsum(
        "ngb,bh->ngh", twist_re, sin_two, precision=high
    )
    scale = (outer * inner) ** (-0.5)
    pick_re = jnp.take(final_re.reshape(count, outer * inner), chosen, axis=1) * scale
    pick_im = jnp.take(final_im.reshape(count, outer * inner), chosen, axis=1) * scale
    return (pick_re, pick_im)


def shards(waves, screen, pair_table, plane_map, trial, probe):
    row_waves = collect(waves, "kp", 2)
    k_rows = row_waves.shape[0]
    k_cols = waves.shape[0] * lax.axis_size("ka") // lax.axis_size("kp")
    slab = collect(waves, "ka", 0)
    col_waves = lax.all_to_all(slab, "kp", split_axis=0, concat_axis=2, tiled=True)
    points = row_waves.shape[2]
    inner = min(128, points)
    outer = points // inner
    tables = make_tables(outer, inner)
    chosen = plane_map % outer * inner + plane_map // outer
    planes = plane_map.shape[0]
    width = NV * NC
    pairs = k_rows * k_cols
    high = lax.Precision.HIGHEST
    left = row_waves.astype(jnp.float32)
    right = col_waves.astype(jnp.float32)
    valence = (left[:, None, :NV, None, :] * right[None, :, None, :NV, :]).reshape(
        pairs, NV * NV, points
    )
    conduction = (left[:, None, NV:, None, :] * right[None, :, None, NV:, :]).reshape(
        pairs, NC * NC, points
    )
    density = jnp.concatenate([valence, conduction], axis=1).reshape(
        pairs * (NV * NV + NC * NC), points
    )
    spec_re, spec_im = spectrum(density, tables, chosen, outer, inner)
    spec_both = jnp.concatenate([spec_re, spec_im], axis=1).reshape(
        pairs, NV * NV + NC * NC, 2 * planes
    )
    val_spec = spec_both[:, : NV * NV, :]
    con_spec = spec_both[:, NV * NV :, :]
    weight = jnp.take(screen, pair_table.reshape(pairs), axis=0)
    weight = jnp.concatenate([weight, weight], axis=1)
    con_spec = con_spec * weight[:, None, :]
    kernel = jnp.einsum("pvg,pcg->pvc", val_spec, con_spec, precision=high)
    kernel = kernel.reshape(pairs, NV, NV, NC, NC).transpose(0, 1, 3, 2, 4) / planes
    blocks = kernel.reshape(k_rows, k_cols, width, width)
    trial_full = collect(trial, "ka", 2)
    probe_full = collect(probe, "kp", 2)
    forward_part = jnp.einsum(
        "kjab,jbm->kam", blocks, trial_full.astype(jnp.float32), precision=high
    )
    adjoint_part = jnp.einsum(
        "kjab,kam->jbm", blocks, probe_full.astype(jnp.float32), precision=high
    )
    applied = summed_on_arrival(forward_part, "kp", 2)
    adjoint = summed_on_arrival(adjoint_part, "ka", 2)
    return (applied, adjoint)


def solution(mesh):
    placed = (
        P("ka", None, "kp"),
        P(),
        P("ka", "kp"),
        P(),
        P("kp", None, "ka"),
        P("ka", None, "kp"),
    )
    return jax.shard_map(
        shards,
        mesh=mesh,
        in_specs=placed,
        out_specs=(P("ka", None, "kp"), P("kp", None, "ka")),
        check_vma=False,
    )
```

profile of v0, /device:TPU:1, one launch (start us, length us, event | category | flops | bytes accessed | tf_op | source)
XLA Modules:
  0.0 182.6 jit_solution(14085714789990141446)
XLA Ops:
  2.1 18.2 %all-to-all-start.3 = ((bf16[16,2,256]{2,1,0:T(2,128)(2,1)}), bf16[16,2,256]{2,1,0:T(2,128)(2,1)S(1)}, u32[]{:S(2)}, u32[]{:S(2)}) async-start(bf16[16,2,256]{2,1,0:T(2,128)(2,1)} %reshape.184), calls=%async_computation.3 | async-start | bytes 32768 | tf_op jit(solution)/shard_map/all_to_all | solution.py:14
  22.3 11.6 %all-to-all-done.3 = bf16[16,2,256]{2,1,0:T(2,128)(2,1)S(1)} async-done(((bf16[16,2,256]{2,1,0:T(2,128)(2,1)}), bf16[16,2,256]{2,1,0:T(2,128)(2,1)S(1)}, u32[]{:S(2)}, u32[]{:S(2)}) %all-to-all-start.3) | async-done | bytes 16416 | tf_op jit(solution)/shard_map/all_to_all | solution.py:14
  34.6 3.5 %all-to-all-start.1 = ((bf16[16,2,16,128]{3,1,2,0:T(2,128)(2,1)}), bf16[16,2,16,128]{3,1,2,0:T(2,128)(2,1)S(1)}, u32[]{:S(2)}, u32[]{:S(2)}) async-start(bf16[16,2,16,128]{3,1,2,0:T(2,128)(2,1)} %broadcast_in_dim.24), calls=%async_computation.1 | async-start | bytes 262144 | tf_op jit(solution)/shard_map/all_to_all | solution.py:14
  40.2 12.1 %all-to-all-done.1 = bf16[16,2,16,128]{3,1,2,0:T(2,128)(2,1)S(1)} async-done(((bf16[16,2,16,128]{3,1,2,0:T(2,128)(2,1)}), bf16[16,2,16,128]{3,1,2,0:T(2,128)(2,1)S(1)}, u32[]{:S(2)}, u32[]{:S(2)}) %all-to-all-start.1) | async-done | bytes 131104 | tf_op jit(solution)/shard_map/all_to_all | solution.py:14
  52.3 10.3 %all-to-all-start.5 = ((bf16[32,2,256]{2,1,0:T(2,128)(2,1)}), bf16[32,2,256]{2,1,0:T(2,128)(2,1)S(1)}, u32[]{:S(2)}, u32[]{:S(2)}) async-start(bf16[32,2,256]{2,1,0:T(2,128)(2,1)} %reshape.188), calls=%async_computation.5 | async-start | bytes 65536 | tf_op jit(solution)/shard_map/all_to_all | solution.py:14
  64.0 6.3 %all-to-all-done.5 = bf16[32,2,256]{2,1,0:T(2,128)(2,1)S(1)} async-done(((bf16[32,2,256]{2,1,0:T(2,128)(2,1)}), bf16[32,2,256]{2,1,0:T(2,128)(2,1)S(1)}, u32[]{:S(2)}, u32[]{:S(2)}) %all-to-all-start.5) | async-done | bytes 32800 | tf_op jit(solution)/shard_map/all_to_all | solution.py:14
  70.3 3.9 %all-to-all-start.2 = ((bf16[32,16,128]{2,1,0:T(8,128)(2,1)}), bf16[32,16,128]{2,1,0:T(8,128)(2,1)S(1)}, u32[]{:S(2)}, u32[]{:S(2)}) async-start(bf16[32,16,128]{2,1,0:T(8,128)(2,1)} %bitcast.2), calls=%async_computation.2 | async-start | bytes 262144 | tf_op jit(solution)/shard_map/all_to_all | solution.py:89
  74.6 8.2 %all-to-all-done.2 = bf16[32,16,128]{2,1,0:T(8,128)(2,1)S(1)} async-done(((bf16[32,16,128]{2,1,0:T(8,128)(2,1)}), bf16[32,16,128]{2,1,0:T(8,128)(2,1)S(1)}, u32[]{:S(2)}, u32[]{:S(2)}) %all-to-all-start.2) | async-done | bytes 131104 | tf_op jit(solution)/shard_map/all_to_all | solution.py:89
  82.8 1.4 broadcast_in_dim.23
  84.2 4.0 %all-to-all-start = ((bf16[32,2,16,128]{3,2,1,0:T(8,128)(2,1)}), bf16[32,2,16,128]{3,2,1,0:T(8,128)(2,1)S(1)}, u32[]{:S(2)}, u32[]{:S(2)}) async-start(bf16[32,2,16,128]{3,2,1,0:T(8,128)(2,1)} %broadcast_in_dim.23), calls=%async_computation | async-start | bytes 524288 | tf_op jit(solution)/shard_map/all_to_all | solution.py:14
  88.6 10.6 %all-to-all-done = bf16[32,2,16,128]{3,2,1,0:T(8,128)(2,1)S(1)} async-done(((bf16[32,2,16,128]{3,2,1,0:T(8,128)(2,1)}), bf16[32,2,16,128]{3,2,1,0:T(8,128)(2,1)S(1)}, u32[]{:S(2)}, u32[]{:S(2)}) %all-to-all-start) | async-done | bytes 262176 | tf_op jit(solution)/shard_map/all_to_all | solution.py:14
  100.9 4.1 %fusion.45 = f32[256,128,32]{1,2,0:T(8,128)S(1)} fusion(f32[256,32,128]{2,1,0:T(8,128)S(1)} %bitcast.132), kind=kOutput, calls=%fused_computation.70 | convolution fusion | flops 402667520 | bytes 8388608 | tf_op jit(solution)/shard_map/ga,nab->ngb/dot_general | solution.py:69
  105.0 4.9 %fusion = (f32[256,32,128]{2,1,0:T(8,128)S(1)}, f32[256,32,128]{2,1,0:T(8,128)S(1)}) fusion(f32[256,128,32]{1,2,0:T(8,128)S(1)} %fusion.45, f32[32,128]{1,0:T(8,128)S(1)} %get-tuple-element.15, f32[32,128]{1,0:T(8,128)S(1)} %get-tuple-element.16, f32[256,32,128]{2,1,0:T(8,128)S(1)} %bitcast.133), kind=kOutput, calls=%fused_computation.6 | convolution fusion | flops 410007552 | bytes 16809984 | tf_op jit(solution)/shard_map/ga,nab->ngb/dot_general | solution.py:68
  109.9 6.6 %fusion.2 = f32[256,32,128]{0,2,1:T(8,128)S(1)} fusion(f32[256,32,128]{2,1,0:T(8,128)S(1)} %get-tuple-element.6), kind=kOutput, calls=%fused_computation.10 | convolution fusion | flops 1610842112 | bytes 8388608 | tf_op jit(solution)/shard_map/ngb,bh->ngh/dot_general | solution.py:75
  116.5 6.6 %fusion.4 = f32[256,32,128]{0,2,1:T(8,128)S(1)} fusion(f32[256,32,128]{2,1,0:T(8,128)S(1)} %get-tuple-element.6), kind=kOutput, calls=%fused_computation.12 | convolution fusion | flops 1610842112 | bytes 8388608 | tf_op jit(solution)/shard_map/ngb,bh->ngh/dot_general | solution.py:72
  123.2 8.8 %fusion.13 = f32[256,32,128]{0,2,1:T(8,128)} fusion(f32[256,32,128]{0,2,1:T(8,128)S(1)} %fusion.2, f32[256,32,128]{2,1,0:T(8,128)S(1)} %get-tuple-element.5), kind=kOutput, calls=%fused_computation.19 | convolution fusion | flops 1611890688 | bytes 12582912 | tf_op jit(solution)/shard_map/ngb,bh->ngh/dot_general | solution.py:75
  131.9 8.6 %fusion.10 = f32[256,32,128]{0,2,1:T(8,128)} fusion(f32[256,32,128]{0,2,1:T(8,128)S(1)} %fusion.4, f32[256,32,128]{2,1,0:T(8,128)S(1)} %get-tuple-element.5), kind=kOutput, calls=%fused_computation.18 | convolution fusion | flops 1611890688 | bytes 12582912 | tf_op jit(solution)/shard_map/ngb,bh->ngh/dot_general | solution.py:72
  140.5 3.8 %gather_fusion.2 = f32[512,256]{1,0:T(8,128)S(1)} fusion(f32[256,4096]{0,1:T(8,128)} %bitcast.135, s32[1024]{0:T(1024)S(1)} %pad_clamp_fusion.1), kind=kCustom, calls=%fused_computation.1.clone | custom fusion | bytes 1050624 | tf_op jit(solution)/shard_map/jit(_take)/gather | solution.py:80
  144.3 3.8 %gather_fusion.1 = f32[512,256]{1,0:T(8,128)S(1)} fusion(f32[256,4096]{0,1:T(8,128)} %bitcast.134, s32[1024]{0:T(1024)S(1)} %pad_clamp_fusion.1), kind=kCustom, calls=%fused_computation.clone | custom fusion | bytes 1050624 | tf_op jit(solution)/shard_map/jit(_take)/gather | solution.py:79
  150.8 3.5 %all-to-all-start.6 = ((f32[16,1,512]{2,1,0:T(1,128)}), f32[16,1,512]{2,1,0:T(1,128)S(1)}, u32[]{:S(2)}, u32[]{:S(2)}) async-start(f32[16,1,512]{2,1,0:T(1,128)} %reshape.190), calls=%async_computation.6 | async-start | bytes 65536 | tf_op jit(solution)/shard_map/all_to_all | solution.py:36
  155.4 12.6 %all-to-all-done.6 = f32[16,1,512]{2,1,0:T(1,128)S(1)} async-done(((f32[16,1,512]{2,1,0:T(1,128)}), f32[16,1,512]{2,1,0:T(1,128)S(1)}, u32[]{:S(2)}, u32[]{:S(2)}) %all-to-all-start.6) | async-done | bytes 32800 | tf_op jit(solution)/shard_map/all_to_all | solution.py:36
  168.0 5.0 %all-to-all-start.4 = ((f32[32,1,512]{2,1,0:T(1,128)}), f32[32,1,512]{2,1,0:T(1,128)S(1)}, u32[]{:S(2)}, u32[]{:S(2)}) async-start(f32[32,1,512]{2,1,0:T(1,128)} %reshape.186), calls=%async_computation.4 | async-start | bytes 131072 | tf_op jit(solution)/shard_map/all_to_all | solution.py:36
  174.9 5.9 %all-to-all-done.4 = f32[32,1,512]{2,1,0:T(1,128)S(1)} async-done(((f32[32,1,512]{2,1,0:T(1,128)}), f32[32,1,512]{2,1,0:T(1,128)S(1)}, u32[]{:S(2)}, u32[]{:S(2)}) %all-to-all-start.4) | async-done | bytes 65568 | tf_op jit(solution)/shard_map/all_to_all | solution.py:36
  180.8 0.8 reduce.1
  (52 shorter events, 16.4 us)
Async XLA Ops:
  0.6 38.3 %copy-start = (f32[32,512]{1,0:T(8,128)S(1)}, f32[32,512]{1,0:T(8,128)}, u32[]{:S(2)}) copy-start(f32[32,512]{1,0:T(8,128)} %param.9) | copy-start | bytes 196612
  2.1 31.9 %all-to-all-start.3 = ((bf16[16,2,256]{2,1,0:T(2,128)(2,1)}), bf16[16,2,256]{2,1,0:T(2,128)(2,1)S(1)}, u32[]{:S(2)}, u32[]{:S(2)}) async-start(bf16[16,2,256]{2,1,0:T(2,128)(2,1)} %reshape.184), calls=%async_computation.3 | async-start | bytes 32768 | tf_op jit(solution)/shard_map/all_to_all | solution.py:14
  34.6 17.7 %all-to-all-start.1 = ((bf16[16,2,16,128]{3,1,2,0:T(2,128)(2,1)}), bf16[16,2,16,128]{3,1,2,0:T(2,128)(2,1)S(1)}, u32[]{:S(2)}, u32[]{:S(2)}) async-start(bf16[16,2,16,128]{3,1,2,0:T(2,128)(2,1)} %broadcast_in_dim.24), calls=%async_computation.1 | async-start | bytes 262144 | tf_op jit(solution)/shard_map/all_to_all | solution.py:14
  52.3 17.9 %all-to-all-start.5 = ((bf16[32,2,256]{2,1,0:T(2,128)(2,1)}), bf16[32,2,256]{2,1,0:T(2,128)(2,1)S(1)}, u32[]{:S(2)}, u32[]{:S(2)}) async-start(bf16[32,2,256]{2,1,0:T(2,128)(2,1)} %reshape.188), calls=%async_computation.5 | async-start | bytes 65536 | tf_op jit(solution)/shard_map/all_to_all | solution.py:14
  70.3 12.5 %all-to-all-start.2 = ((bf16[32,16,128]{2,1,0:T(8,128)(2,1)}), bf16[32,16,128]{2,1,0:T(8,128)(2,1)S(1)}, u32[]{:S(2)}, u32[]{:S(2)}) async-start(bf16[32,16,128]{2,1,0:T(8,128)(2,1)} %bitcast.2), calls=%async_computation.2 | async-start | bytes 262144 | tf_op jit(solution)/shard_map/all_to_all | solution.py:89
  84.2 15.0 %all-to-all-start = ((bf16[32,2,16,128]{3,2,1,0:T(8,128)(2,1)}), bf16[32,2,16,128]{3,2,1,0:T(8,128)(2,1)S(1)}, u32[]{:S(2)}, u32[]{:S(2)}) async-start(bf16[32,2,16,128]{3,2,1,0:T(8,128)(2,1)} %broadcast_in_dim.23), calls=%async_computation | async-start | bytes 524288 | tf_op jit(solution)/shard_map/all_to_all | solution.py:14
  150.8 17.1 %all-to-all-start.6 = ((f32[16,1,512]{2,1,0:T(1,128)}), f32[16,1,512]{2,1,0:T(1,128)S(1)}, u32[]{:S(2)}, u32[]{:S(2)}) async-start(f32[16,1,512]{2,1,0:T(1,128)} %reshape.190), calls=%async_computation.6 | async-start | bytes 65536 | tf_op jit(solution)/shard_map/all_to_all | solution.py:36
  168.0 12.9 %all-to-all-start.4 = ((f32[32,1,512]{2,1,0:T(1,128)}), f32[32,1,512]{2,1,0:T(1,128)S(1)}, u32[]{:S(2)}, u32[]{:S(2)}) async-start(f32[32,1,512]{2,1,0:T(1,128)} %reshape.186), calls=%async_computation.4 | async-start | bytes 131072 | tf_op jit(solution)/shard_map/all_to_all | solution.py:36
where the time goes:
time: 186 us; the launch traced here: 183 us
  waiting for transfers between devices  67.3 us (36%)
  starting transfers between devices  48.4 us (26%)
  matrix products  40.6 us (22%)
  local copies, waits for them, and re-layouts  19 us (10%)
  other arithmetic  6.06 us (3%)
    all_to_all x4, waiting for transfers between devices, from_everyone(): lax.all_to_all(jnp.broadcast_to(x[None], (count, *x.shape)), axis, 0, 0,...  40.6 us
    all_to_all x4, starting transfers between devices, from_everyone(): lax.all_to_all(jnp.broadcast_to(x[None], (count, *x.shape)), axis, 0, 0,...  36 us
    all_to_all x2, waiting for transfers between devices, summed_on_arrival(): lax.all_to_all(tiles, axis, split_axis=0, concat_axis=0, tiled=True)  18.5 us
    dot_general x1, matrix products, spectrum(): jnp.einsum('ngb,bh->ngh', twist_re, sin_two, precision=high)  8.75 us
    dot_general x1, matrix products, spectrum(): jnp.einsum('ngb,bh->ngh', twist_re, cos_two, precision=high)  8.61 us
    all_to_all x2, starting transfers between devices, summed_on_arrival(): lax.all_to_all(tiles, axis, split_axis=0, concat_axis=0, tiled=True)  8.5 us
    all_to_all x1, waiting for transfers between devices, shards(): lax.all_to_all(slab, 'kp', split_axis=0, concat_axis=2, tiled=True)  8.24 us
    dot_general x1, matrix products, spectrum(): jnp.einsum('ngb,bh->ngh', twist_im, sin_two, precision=high)  6.63 us
  transfers between devices with their start and end apart: 7, of which 7 were waited for; matrix products, arithmetic and copies ran while one was open for 5% of the time, Pallas kernels for 0%

commit v1 on v0

v1 whole, which is shorter than its diff:
```python
import math

import jax
import jax.numpy as jnp
import numpy as np
from jax import lax
from jax.experimental import pallas as pl
from jax.experimental.pallas import tpu as pltpu
from jax.sharding import PartitionSpec as P

NV = 8
NC = 8
OUTER = 32
INNER = 128
BLOCK = 56
SLAB = 40
GROUPS = OUTER // 2 + 1
BF = jnp.bfloat16
F32 = jnp.float32


def split_np(values):
    high = np.asarray(values, np.float32).astype(jnp.bfloat16)
    low = (np.asarray(values, np.float64) - high.astype(np.float64)).astype(jnp.bfloat16)
    return high, low


def constants():
    inner = np.arange(INNER)
    angle = 2.0 * np.pi * ((inner[:, None] * inner[None, :]) % INNER) / INNER
    cos, sin = np.cos(angle), np.sin(angle)
    matrix = np.block([[cos, -sin], [sin, cos]])
    high, low = split_np(matrix)
    group = np.arange(GROUPS)
    twist = 2.0 * np.pi * (group[:, None] * inner[None, :]) / (OUTER * INNER)
    table = np.stack([np.cos(twist), np.sin(twist)], axis=1).reshape(2 * GROUPS, 1, INNER)
    table = np.broadcast_to(table, (2 * GROUPS, 8, INNER)).astype(np.float32)
    rows = np.arange(128)
    halves = np.arange(64)
    place = np.zeros((2, 128, 64), np.float32)
    for half in range(2):
        place[half] = rows[:, None] == (halves // 4 * 8 + half * 4 + halves % 4)[None, :]
    lane = np.arange(8 * 64)
    pick = np.arange(64)
    spread = (pick[:, None] // 8 == lane[None, :] // 64) & (pick[:, None] % 8 == lane[None, :] % 8)
    keep = (rows[:, None] % 8) == (lane[None, :] % 64 // 8)
    return (
        high,
        low,
        np.ascontiguousarray(table),
        place.astype(jnp.bfloat16),
        np.ascontiguousarray(np.swapaxes(place, 1, 2)).astype(jnp.bfloat16),
        spread.astype(jnp.bfloat16),
        keep.astype(np.float32),
    )


def real_fft(x):
    n = len(x)
    if n == 2:
        return [x[0] + x[1], x[0] - x[1]], [None, None]
    even_re, even_im = real_fft(x[0::2])
    odd_re, odd_im = real_fft(x[1::2])
    half = n // 2
    out_re, out_im = [None] * (half + 1), [None] * (half + 1)
    out_re[0] = even_re[0] + odd_re[0]
    out_re[half] = even_re[0] - odd_re[0]
    out_re[half // 2] = even_re[half // 2]
    out_im[half // 2] = -odd_re[half // 2]
    for k in range(1, half // 2):
        c, s = math.cos(2 * math.pi * k / n), math.sin(2 * math.pi * k / n)
        if 8 * k == n:
            turn_re = (odd_re[k] + odd_im[k]) * c
            turn_im = (odd_im[k] - odd_re[k]) * c
        else:
            turn_re = odd_re[k] * c + odd_im[k] * s
            turn_im = odd_im[k] * c - odd_re[k] * s
        out_re[k] = even_re[k] + turn_re
        out_im[k] = even_im[k] + turn_im
        out_re[half - k] = even_re[k] - turn_re
        out_im[half - k] = turn_im - even_im[k]
    return out_re, out_im


def split(x):
    high = x.astype(BF)
    return high, (x - high.astype(F32)).astype(BF)


def dot(a, b):
    return lax.dot_general(a, b, (((1,), (0,)), ((), ())), preferred_element_type=F32)


def dot_t(a, b):
    return lax.dot_general(a, b, (((1,), (1,)), ((), ())), preferred_element_type=F32)


def block_kernel(
    data, trial, weight, high, low, table, place, gather, spread, keep, applied, adjoint, wide, grid, acc
):
    wide[...] = data[:, :48, :].astype(F32)

    def transform(i, carry):
        side = pl.multiple_of(32 + (i // 8) % 2 * 8, 8)
        base = pl.multiple_of(i * 8, 8)
        tiles = [
            jnp.broadcast_to(wide[a, pl.ds(i, 1), :], (8, INNER)) * wide[a, pl.ds(side, 8), :] for a in range(OUTER)
        ]
        re, im = real_fft(tiles)
        for c in range(GROUPS):
            if c == 0:
                new_re, new_im = re[0], jnp.zeros_like(re[0])
            elif c == GROUPS - 1:
                new_re, new_im = re[c] * table[2 * c], -(re[c] * table[2 * c + 1])
            else:
                cos, sin = table[2 * c], table[2 * c + 1]
                new_re = re[c] * cos + im[c] * sin
                new_im = im[c] * cos - re[c] * sin
            grid[c, pl.ds(base, 8), :INNER] = new_re
            grid[c, pl.ds(base, 8), INNER:] = new_im
        return carry

    lax.fori_loop(0, 32, transform, 0)
    acc[...] = jnp.zeros_like(acc)

    def contract(c, carry):
        x_high, x_low = split(grid[c])
        s = dot(x_high, high[...]) + dot(x_low, high[...]) + dot(x_high, low[...])
        for q in range(2):
            val = s[q * 128 : q * 128 + 64]
            con = s[q * 128 + 64 : q * 128 + 128]
            w = weight[q, pl.ds(c, 1), :]
            con = con * jnp.concatenate([w, w], axis=1)
            val = jnp.concatenate(split(val), axis=0)
            con = jnp.concatenate(split(con), axis=0)
            acc[q] += dot_t(val, con)
        return carry

    lax.fori_loop(0, GROUPS, contract, 0)

    pair = []
    for q in range(2):
        total = acc[q]
        pair.append(total[:64, :64] + total[:64, 64:] + total[64:, :64] + total[64:, 64:])
    both = jnp.concatenate(pair, axis=0)
    both_high, both_low = split(both)
    moved = (dot(both_high, spread[...]) + dot(both_low, spread[...])) * keep[...]
    moved = moved.reshape(16, 8, 512).sum(axis=1)
    parts = [moved[q * 8 : q * 8 + 8, x * 64 : x * 64 + 64] for q in range(2) for x in range(8)]
    kernel_high, kernel_low = split(jnp.concatenate(parts, axis=0))

    packed = trial[...].astype(BF)
    columns = (dot(place[0], packed[:, :64]) + dot(place[1], packed[:, 64:])).astype(BF)
    applied[...] = dot_t(columns, kernel_high) + dot_t(columns, kernel_low)

    probe = data[:, 48:52, :].reshape(128, 128)
    sides = []
    for half in range(2):
        chosen = dot(gather[half], probe).astype(BF)
        sides.append(dot(chosen, kernel_high) + dot(chosen, kernel_low))
    adjoint[...] = jnp.concatenate(sides, axis=1)


def make_weight(screen, pair_table, plane_map, planes, points):
    chosen = jnp.take(screen, pair_table.reshape(-1), axis=0) * (1.0 / (planes * points))
    group = jnp.arange(GROUPS, dtype=jnp.int32)[:, None]
    other = points - plane_map
    direct = (plane_map % OUTER)[None, :] == group
    mirror = ((other % OUTER)[None, :] == group) & (group > 0) & (group < GROUPS - 1)
    mask = jnp.concatenate([direct, mirror], axis=1).astype(F32)
    left = mask[None] * jnp.concatenate([chosen, chosen], axis=1)[:, None, :]
    spot = jnp.concatenate([plane_map // OUTER, other // OUTER])
    right = (spot[None, :] == jnp.arange(INNER, dtype=jnp.int32)[:, None]).astype(F32)
    return jnp.einsum("qcg,hg->qch", left, right, precision=lax.Precision.HIGHEST)


def local_blocks(data, trial, weight, call=pl.pallas_call):
    vmem = pl.BlockSpec(memory_space=pltpu.VMEM)
    return call(
        block_kernel,
        out_shape=(
            jax.ShapeDtypeStruct((128, 128), F32),
            jax.ShapeDtypeStruct((64, 128), F32),
        ),
        in_specs=[vmem] * 10,
        out_specs=(vmem, vmem),
        scratch_shapes=[
            pltpu.VMEM((OUTER, 48, INNER), F32),
            pltpu.VMEM((GROUPS, 256, 2 * INNER), F32),
            pltpu.VMEM((2, 128, 128), F32),
        ],
        compiler_params=pltpu.CompilerParams(vmem_limit_bytes=32 << 20),
        name="pair_blocks",
    )(data, trial, weight, *constants())


def shards(waves, screen, pair_table, plane_map, trial, probe):
    n_rows = lax.axis_size("ka")
    n_cols = lax.axis_size("kp")
    own = waves.reshape(32, INNER)
    trial_rows = trial.reshape(64, 2, 4).transpose(2, 1, 0).reshape(4, 128)
    probe_rows = probe.reshape(2, 8, 8, 4).transpose(3, 0, 2, 1).reshape(4, 128)
    blank = jnp.zeros((4, 128), BF)

    out = jnp.concatenate([own, trial_rows, blank], axis=0)
    out = jnp.broadcast_to(out[None], (n_rows, SLAB, 128))
    slab = lax.all_to_all(out, "ka", 0, 0, tiled=True)
    trial_full = slab[:, 32:36, :].reshape(64, 128)
    partner = slab[:, :32, :].reshape(n_cols, 16, 128)

    shared = jnp.concatenate([own, probe_rows, blank], axis=0)
    shared = jnp.broadcast_to(shared[None], (n_cols, 40, 128))
    out = jnp.concatenate([shared[:, :32], partner, shared[:, 32:]], axis=1)
    data = lax.all_to_all(out, "kp", 0, 0, tiled=True)

    weight = make_weight(screen, pair_table, plane_map, plane_map.shape[0], OUTER * INNER)
    applied, adjoint = local_blocks(data, trial_full, weight)

    applied = lax.all_to_all(applied.reshape(n_cols, 4, 128), "kp", 0, 0, tiled=True).sum(axis=0)
    adjoint = lax.all_to_all(adjoint.reshape(n_rows, 4, 128), "ka", 0, 0, tiled=True).sum(axis=0)
    applied = applied.reshape(4, 2, 8, 8).transpose(1, 3, 2, 0).reshape(2, 64, 4)
    adjoint = adjoint.reshape(4, 2, 64).transpose(2, 1, 0).reshape(1, 64, 8)
    return applied, adjoint


def solution(mesh):
    placed = (
        P("ka", None, "kp"),
        P(),
        P("ka", "kp"),
        P(),
        P("kp", None, "ka"),
        P("ka", None, "kp"),
    )
    return jax.shard_map(
        shards,
        mesh=mesh,
        in_specs=placed,
        out_specs=(P("ka", None, "kp"), P("kp", None, "ka")),
        check_vma=False,
    )
```

time: 186 us -> 107 us (0.58); the launches traced: 183 us -> 106 us
  matrix products: 40.6 us -> 0.4 us
  waiting for transfers between devices: 67.3 us -> 34.3 us
  blocking collectives: 0 us -> 16.5 us
  starting transfers between devices: 48.4 us -> 35.2 us
  local copies, waits for them, and re-layouts: 19 us -> 6.21 us
  Pallas kernels: 0 us -> 11.5 us
  other arithmetic: 6.06 us -> 1.17 us
    dot_general x9 -> x1, matrix products: 40.6 us -> 0.4 us  [make_weight(): jnp.einsum('qcg,hg->qch', left, right, precision=lax.Precision.HIGHEST)]
    all_to_all x7 -> x3, waiting for transfers between devices: 67.3 us -> 34.3 us  [the longest x1 13.8 us: shards(): data = lax.all_to_all(out, 'kp', 0, 0, tiled=True)]
    all_to_all x0 -> x1, blocking collectives: none -> 16.5 us  [shards(): lax.all_to_all(adjoint.reshape(n_rows, 4, 128), 'ka', 0, 0, tiled=True)]
    all_to_all x7 -> x3, starting transfers between devices: 48.4 us -> 35.2 us  [the longest x1 18.3 us: shards(): slab = lax.all_to_all(out, 'ka', 0, 0, tiled=True)]
    pallas_call x0 -> x1, Pallas kernels: none -> 11.5 us  [local_blocks(): call(block_kernel, out_shape=(jax.ShapeDtypeStruct((128, 128), F32), jax....]
    gather x3 -> x1, local copies, waits for them, and re-layouts: 8.07 us -> 0.56 us  [make_weight(): jnp.take(screen, pair_table.reshape(-1), axis=0) * (1.0 / (planes * points))]
    unnamed x15 -> x28, local copies, waits for them, and re-layouts: 6.35 us -> 1.36 us
  transfers between devices with their start and end apart: 7 -> 3, of which waited for: 7 -> 3; matrix products, arithmetic and copies ran while one was open for 5% -> 2% of each run, Pallas kernels for 0% -> 0%
where the time goes in v1:
time: 107 us; the launch traced here: 106 us
  starting transfers between devices  35.2 us (33%)
  waiting for transfers between devices  34.3 us (32%)
  blocking collectives  16.5 us (15%)
  Pallas kernels  11.5 us (11%)
  local copies, waits for them, and re-layouts  6.21 us (6%)
  other arithmetic  1.17 us (1%)
    all_to_all x1, starting transfers between devices, shards(): slab = lax.all_to_all(out, 'ka', 0, 0, tiled=True)  18.3 us
    all_to_all x1, blocking collectives, shards(): lax.all_to_all(adjoint.reshape(n_rows, 4, 128), 'ka', 0, 0, tiled=True)  16.5 us
    all_to_all x1, waiting for transfers between devices, shards(): data = lax.all_to_all(out, 'kp', 0, 0, tiled=True)  13.8 us
    all_to_all x1, waiting for transfers between devices, shards(): slab = lax.all_to_all(out, 'ka', 0, 0, tiled=True)  13.5 us
    pallas_call x1, Pallas kernels, local_blocks(): call(block_kernel, out_shape=(jax.ShapeDtypeStruct((128, 128), F32), jax....  11.5 us
    all_to_all x1, starting transfers between devices, shards(): data = lax.all_to_all(out, 'kp', 0, 0, tiled=True)  11.4 us
    all_to_all x1, waiting for transfers between devices, shards(): lax.all_to_all(applied.reshape(n_cols, 4, 128), 'kp', 0, 0, tiled=True)  7.03 us
    all_to_all x1, starting transfers between devices, shards(): lax.all_to_all(applied.reshape(n_cols, 4, 128), 'kp', 0, 0, tiled=True)  5.42 us
  transfers between devices with their start and end apart: 3, of which 3 were waited for; matrix products, arithmetic and copies ran while one was open for 2% of the time, Pallas kernels for 0%

profile of v1, /device:TPU:1, one launch (start us, length us, event | category | flops | bytes accessed | tf_op | source)
XLA Modules:
  0.0 106.1 jit_solution(10589521219855568497)
XLA Ops:
  0.7 0.7 copy.19
  1.4 0.1 reshape.106
  1.6 0.7 broadcast_in_dim.20
  2.3 18.3 %all-to-all-start = ((bf16[16,40,128]{2,1,0:T(8,128)(2,1)}), bf16[16,40,128]{2,1,0:T(8,128)(2,1)S(1)}, u32[]{:S(2)}, u32[]{:S(2)}) async-start(bf16[16,40,128]{2,1,0:T(8,128)(2,1)} %broadcast_in_dim.20), calls=%async_computation | async-start | bytes 327680 | tf_op jit(solution)/shard_map/all_to_all | solution.py:207
  20.6 0.1 reshape.108
  20.7 0.1 copy.20
  20.8 0.1 reshape.109
  20.9 0.6 copy-done.13
  21.6 13.5 %all-to-all-done = bf16[16,40,128]{2,1,0:T(8,128)(2,1)S(1)} async-done(((bf16[16,40,128]{2,1,0:T(8,128)(2,1)}), bf16[16,40,128]{2,1,0:T(8,128)(2,1)S(1)}, u32[]{:S(2)}, u32[]{:S(2)}) %all-to-all-start) | async-done | bytes 163872 | tf_op jit(solution)/shard_map/all_to_all | solution.py:207
  35.1 0.7 copy-done.8
  35.8 0.9 slice-done
  36.6 0.8 pad_maximum_fusion
  37.5 11.4 %all-to-all-start.1 = ((bf16[32,56,128]{2,1,0:T(8,128)(2,1)}), bf16[32,56,128]{2,1,0:T(8,128)(2,1)S(1)}, u32[]{:S(2)}, u32[]{:S(2)}) async-start(bf16[32,56,128]{2,1,0:T(8,128)(2,1)} %pad_maximum_fusion), calls=%async_computation.1 | async-start | bytes 917504 | tf_op jit(solution)/shard_map/all_to_all | solution.py:214
  49.0 0.6 gather_fusion
  49.8 0.4 fusion.1.weight
  50.2 13.8 %all-to-all-done.1.data = bf16[32,56,128]{2,1,0:T(8,128)(2,1)S(1)} async-done(((bf16[32,56,128]{2,1,0:T(8,128)(2,1)}), bf16[32,56,128]{2,1,0:T(8,128)(2,1)S(1)}, u32[]{:S(2)}, u32[]{:S(2)}) %all-to-all-start.1) | async-done | bytes 458784 | tf_op jit(solution)/shard_map/all_to_all | solution.py:214
  64.1 11.5 %pair_blocks.1 = (f32[128,128]{1,0:T(8,128)}, f32[64,128]{1,0:T(8,128)S(1)}) custom-call(bf16[32,56,128]{2,1,0:T(8,128)(2,1)S(1)} %all-to-all-done.1.data, bf16[64,128]{1,0:T(8,128)(2,1)S(1)} %bitcast.27, f32[2,17,128]{2,1,0:T(8,128)S(1)} %fusion.1.weight, bf16[256,256]{1,0:T(8,128)(2,1)S(1)} %copy-done.4, bf16[256,256]{1,0:T(8,128)(2,1)S(1)} %copy-done.3, ...), custom_call_target="tpu_custom_call" | custom-call | tf_op jit(solution)/shard_map/pair_blocks/pallas_call | solution.py:179
  75.5 16.5 %all_to_all.20 = f32[16,4,128]{2,1,0:T(4,128)S(1)} all-to-all(f32[16,4,128]{2,1,0:T(4,128)S(1)} %bitcast.28), channel_id=1, replica_groups=mesh['ka'=16,'kp'=32] {'ka'}, dimensions={0} | all-to-all | bytes 65536 | tf_op jit(solution)/shard_map/all_to_all | solution.py:220
  92.0 5.4 %all-to-all-start.2 = ((f32[32,4,128]{2,1,0:T(4,128)}), f32[32,4,128]{2,1,0:T(4,128)S(1)}, u32[]{:S(2)}, u32[]{:S(2)}) async-start(f32[32,4,128]{2,1,0:T(4,128)} %bitcast.9), calls=%async_computation.2 | async-start | bytes 131072 | tf_op jit(solution)/shard_map/all_to_all | solution.py:219
  97.4 0.1 reshape.115
  97.5 0.6 copy.22
  98.1 7.0 %all-to-all-done.2 = f32[32,4,128]{2,1,0:T(4,128)S(1)} async-done(((f32[32,4,128]{2,1,0:T(4,128)}), f32[32,4,128]{2,1,0:T(4,128)S(1)}, u32[]{:S(2)}, u32[]{:S(2)}) %all-to-all-start.2) | async-done | bytes 65568 | tf_op jit(solution)/shard_map/all_to_all | solution.py:219
  105.2 0.1 reshape.112
  105.4 0.7 reshape.113
  (48 shorter events, 0.7 us)
Async XLA Ops:
  0.6 48.3 %copy-start = (f32[32,512]{1,0:T(8,128)S(1)}, f32[32,512]{1,0:T(8,128)}, u32[]{:S(2)}) copy-start(f32[32,512]{1,0:T(8,128)} %param.14) | copy-start | bytes 196612
  0.6 0.9 copy-start.10
  2.3 18.3 %copy-start.11 = (bf16[2,64,4]{1,2,0:T(4,128)(2,1)S(1)}, bf16[2,64,4]{1,2,0:T(4,128)(2,1)}, u32[]{:S(2)}) copy-start(bf16[2,64,4]{1,2,0:T(4,128)(2,1)} %param.18) | copy-start | bytes 3076
  2.3 32.7 %all-to-all-start = ((bf16[16,40,128]{2,1,0:T(8,128)(2,1)}), bf16[16,40,128]{2,1,0:T(8,128)(2,1)S(1)}, u32[]{:S(2)}, u32[]{:S(2)}) async-start(bf16[16,40,128]{2,1,0:T(8,128)(2,1)} %broadcast_in_dim.20), calls=%async_computation | async-start | bytes 327680 | tf_op jit(solution)/shard_map/all_to_all | solution.py:207
  20.9 0.7 copy-start.13
  35.0 0.7 copy-start.8
  35.7 0.9 slice-start
  37.4 12.1 %copy-start.12 = (s32[512]{0:T(512)S(1)}, s32[512]{0:T(512)}, u32[]{:S(2)}) copy-start(s32[512]{0:T(512)} %param.16) | copy-start | bytes 6148
  37.4 12.8 %copy-start.9 = (bf16[16,40,128]{2,1,0:T(8,128)(2,1)S(1)}, bf16[16,40,128]{2,1,0:T(8,128)(2,1)}, u32[]{:S(2)}) copy-start(bf16[16,40,128]{2,1,0:T(8,128)(2,1)} %copy-done.8) | copy-start | bytes 491524
  37.4 26.6 %copy-start.3 = (bf16[256,256]{1,0:T(8,128)(2,1)S(1)}, bf16[256,256]{1,0:T(8,128)(2,1)}, u32[]{:S(2)}) copy-start(bf16[256,256]{1,0:T(8,128)(2,1)} %constant.79.clone.low) | copy-start | bytes 393220
  37.4 26.6 %copy-start.4 = (bf16[256,256]{1,0:T(8,128)(2,1)S(1)}, bf16[256,256]{1,0:T(8,128)(2,1)}, u32[]{:S(2)}) copy-start(bf16[256,256]{1,0:T(8,128)(2,1)} %constant.78.clone.high) | copy-start | bytes 393220
  37.4 26.6 %copy-start.6 = (bf16[2,128,64]{2,1,0:T(8,128)(2,1)S(1)}, bf16[2,128,64]{2,1,0:T(8,128)(2,1)}, u32[]{:S(2)}) copy-start(bf16[2,128,64]{2,1,0:T(8,128)(2,1)} %constant.81.clone.place) | copy-start | bytes 98308
  37.4 26.6 %copy-start.7 = (bf16[2,64,128]{2,1,0:T(8,128)(2,1)S(1)}, bf16[2,64,128]{2,1,0:T(8,128)(2,1)}, u32[]{:S(2)}) copy-start(bf16[2,64,128]{2,1,0:T(8,128)(2,1)} %constant.82.clone.gather) | copy-start | bytes 98308
  37.5 26.5 %all-to-all-start.1 = ((bf16[32,56,128]{2,1,0:T(8,128)(2,1)}), bf16[32,56,128]{2,1,0:T(8,128)(2,1)S(1)}, u32[]{:S(2)}, u32[]{:S(2)}) async-start(bf16[32,56,128]{2,1,0:T(8,128)(2,1)} %pad_maximum_fusion), calls=%async_computation.1 | async-start | bytes 917504 | tf_op jit(solution)/shard_map/all_to_all | solution.py:214
  48.9 15.1 %copy-start.1 = (f32[128,512]{1,0:T(8,128)S(1)}, f32[128,512]{1,0:T(8,128)}, u32[]{:S(2)}) copy-start(f32[128,512]{1,0:T(8,128)} %constant.84.clone.keep) | copy-start | bytes 786436
  49.8 14.3 %copy-start.2 = (f32[34,8,128]{2,1,0:T(8,128)S(1)}, f32[34,8,128]{2,1,0:T(8,128)}, u32[]{:S(2)}) copy-start(f32[34,8,128]{2,1,0:T(8,128)} %constant.80.clone.table) | copy-start | bytes 417796
  49.8 14.3 %copy-start.5 = (bf16[64,512]{1,0:T(8,128)(2,1)S(1)}, bf16[64,512]{1,0:T(8,128)(2,1)}, u32[]{:S(2)}) copy-start(bf16[64,512]{1,0:T(8,128)(2,1)} %constant.83.clone.spread) | copy-start | bytes 196612
  92.0 13.2 %all-to-all-start.2 = ((f32[32,4,128]{2,1,0:T(4,128)}), f32[32,4,128]{2,1,0:T(4,128)S(1)}, u32[]{:S(2)}, u32[]{:S(2)}) async-start(f32[32,4,128]{2,1,0:T(4,128)} %bitcast.9), calls=%async_computation.2 | async-start | bytes 131072 | tf_op jit(solution)/shard_map/all_to_all | solution.py:219

commit v2 on v1

v2 whole, which is shorter than its diff:
```python
import math

import jax
import jax.numpy as jnp
import numpy as np
from jax import lax
from jax.experimental import pallas as pl
from jax.experimental.pallas import tpu as pltpu
from jax.sharding import PartitionSpec as P

OUTER = 32
INNER = 128
BLOCK = 56
SLAB = 40
GROUPS = OUTER // 2 + 1
UNROLL = 4
BF = jnp.bfloat16
F32 = jnp.float32


def split_np(values):
    high = np.asarray(values, np.float32).astype(jnp.bfloat16)
    low = (np.asarray(values, np.float64) - high.astype(np.float64)).astype(jnp.bfloat16)
    return high, low


def constants():
    inner = np.arange(INNER)
    angle = 2.0 * np.pi * ((inner[:, None] * inner[None, :]) % INNER) / INNER
    cos, sin = np.cos(angle), np.sin(angle)
    high, low = split_np(np.block([[cos, -sin], [sin, cos]]))
    group = np.arange(GROUPS)
    twist = 2.0 * np.pi * (group[:, None] * inner[None, :]) / (OUTER * INNER)
    table = np.stack([np.cos(twist), np.sin(twist)], axis=1).reshape(2 * GROUPS, 1, INNER)
    table = np.broadcast_to(table, (2 * GROUPS, 8, INNER)).astype(np.float32)
    return np.concatenate([high, high, low], axis=0), np.ascontiguousarray(table)


def real_fft(x):
    n = len(x)
    if n == 2:
        return [x[0] + x[1], x[0] - x[1]], [None, None]
    even_re, even_im = real_fft(x[0::2])
    odd_re, odd_im = real_fft(x[1::2])
    half = n // 2
    out_re, out_im = [None] * (half + 1), [None] * (half + 1)
    out_re[0] = even_re[0] + odd_re[0]
    out_re[half] = even_re[0] - odd_re[0]
    out_re[half // 2] = even_re[half // 2]
    out_im[half // 2] = -odd_re[half // 2]
    for k in range(1, half // 2):
        c, s = math.cos(2 * math.pi * k / n), math.sin(2 * math.pi * k / n)
        if 8 * k == n:
            turn_re = (odd_re[k] + odd_im[k]) * c
            turn_im = (odd_im[k] - odd_re[k]) * c
        else:
            turn_re = odd_re[k] * c + odd_im[k] * s
            turn_im = odd_im[k] * c - odd_re[k] * s
        out_re[k] = even_re[k] + turn_re
        out_im[k] = even_im[k] + turn_im
        out_re[half - k] = even_re[k] - turn_re
        out_im[half - k] = turn_im - even_im[k]
    return out_re, out_im


def split(x):
    high = x.astype(BF)
    return high, (x - high.astype(F32)).astype(BF)


def dot(a, b):
    return lax.dot_general(a, b, (((1,), (0,)), ((), ())), preferred_element_type=F32)


def dot_t(a, b):
    return lax.dot_general(a, b, (((1,), (1,)), ((), ())), preferred_element_type=F32)


def first_kernel(own, trial, out):
    rows = jnp.zeros((8, 128 - trial.shape[1]), BF)
    last = jnp.concatenate([trial[...], rows], axis=1)
    for i in range(out.shape[0]):
        out[i, :32, :] = own[...]
        out[i, 32:, :] = last


def second_kernel(own, probe, slab, out):
    for i in range(out.shape[0]):
        out[i, :32, :] = own[...]
        out[i, 32:48, :] = slab[i // 2, i % 2 * 16 : i % 2 * 16 + 16, :]
        out[i, 48:, :] = probe[...]


def last_kernel(parts, out):
    total = parts[...].sum(axis=0)
    out[:4, :] = total[:, :64]
    out[4:, :] = total[:, 64:]


def block_kernel(data, slab, weight, matrix, table, applied, adjoint, wide, grid, val, con, acc):
    wide[...] = data[:, :48, :].astype(F32)

    def transform(i):
        q, t, x = i // 16, i // 8 % 2, i % 8
        single = t * (q * 16 + 8) + (1 - t) * 32 + x
        side = pl.multiple_of(t * 40 + (1 - t) * q * 16, 8)
        base = pl.multiple_of(i * 8, 8)
        tiles = [
            jnp.broadcast_to(wide[a, pl.ds(single, 1), :], (8, INNER)) * wide[a, pl.ds(side, 8), :]
            for a in range(OUTER)
        ]
        re, im = real_fft(tiles)
        for c in range(GROUPS):
            if c == 0:
                new_re, new_im = re[0], jnp.zeros_like(re[0])
            elif c == GROUPS - 1:
                new_re, new_im = re[c] * table[2 * c], -(re[c] * table[2 * c + 1])
            else:
                cos, sin = table[2 * c], table[2 * c + 1]
                new_re = re[c] * cos + im[c] * sin
                new_im = im[c] * cos - re[c] * sin
            grid[c, pl.ds(base, 8), :INNER] = new_re
            grid[c, pl.ds(base, 8), INNER:] = new_im

    def transform_some(i, carry):
        for part in range(UNROLL):
            transform(i * UNROLL + part)
        return carry

    lax.fori_loop(0, 32 // UNROLL, transform_some, 0)
    acc[...] = jnp.zeros_like(acc)

    def spectra(c, count, slot):
        x = grid[pl.ds(c, count)].reshape(count * 256, 256)
        x_high, x_low = split(x)
        s = dot(jnp.concatenate([x_high, x_low, x_high], axis=1), matrix[...])
        for part in range(count):
            for q in range(2):
                w = weight[q, pl.ds(c + part, 1), :]
                w = jnp.concatenate([w, w], axis=1)
                row = part * 256 + q * 128
                lanes = slice(part * 256, part * 256 + 256)
                val[slot, q, :, lanes] = jnp.concatenate(split(s[row : row + 64]), axis=0)
                con[slot, q, :, lanes] = jnp.concatenate(split(s[row + 64 : row + 128] * w), axis=0)

    def contract(slot):
        for q in range(2):
            acc[q] += dot_t(val[slot, q], con[slot, q])

    def four_groups(t, carry):
        spectra(4 * t + 1, 2, 1)
        contract(0)
        spectra(4 * t + 3, 2, 0)
        contract(1)
        return carry

    val[0, :, :, 256:] = jnp.zeros((2, 128, 256), BF)
    con[0, :, :, 256:] = jnp.zeros((2, 128, 256), BF)
    spectra(0, 1, 0)
    lax.fori_loop(0, GROUPS // 4, four_groups, 0)
    contract(0)

    lane = lax.broadcasted_iota(jnp.int32, (64, 128), 1)
    twice = []
    for q in range(2):
        part = acc[q, :64, :] + acc[q, 64:, :]
        twice.append(part + pltpu.roll(part, 64, 1))
    both = jnp.where(lane < 64, twice[0], twice[1])
    spot = lane[:8] // 8 % 8
    rows = []
    for x in range(8):
        row = jnp.zeros((8, 128), F32)
        for w in range(8):
            block = both[w * 8 : w * 8 + 8]
            shift = (w - x) * 8 % 128
            if shift:
                block = pltpu.roll(block, shift, 1)
            row = jnp.where(spot == w, block, row)
        rows.append(row)
    moved = jnp.concatenate(rows, axis=0)
    moved = jnp.concatenate([moved, pltpu.roll(moved, 64, 1)], axis=0)
    high, low = split(moved)

    columns = slab[:, 32:40, :].astype(F32).reshape(128, 128).astype(BF)
    applied[...] = dot_t(columns, high) + dot_t(columns, low)
    probe = data[:, 48:52, :].reshape(128, 128)
    full = dot(probe, high) + dot(probe, low)
    turned = pltpu.roll(pltpu.roll(full, 64, 1), 124, 0)
    wide_lane = lax.broadcasted_iota(jnp.int32, (128, 128), 1)
    full = jnp.where(wide_lane < 64, full, turned).reshape(16, 8, 128)
    adjoint[...] = full[:, :4, :]


def make_weight(screen, pair_table, plane_map, planes, points):
    chosen = jnp.take(screen, pair_table.reshape(-1), axis=0) * (1.0 / (planes * points))
    group = jnp.arange(GROUPS, dtype=jnp.int32)[:, None]
    other = points - plane_map
    direct = (plane_map % OUTER)[None, :] == group
    mirror = ((other % OUTER)[None, :] == group) & (group > 0) & (group < GROUPS - 1)
    mask = jnp.concatenate([direct, mirror], axis=1).astype(F32)
    left = mask[None] * jnp.concatenate([chosen, chosen], axis=1)[:, None, :]
    spot = jnp.concatenate([plane_map // OUTER, other // OUTER])
    right = (spot[None, :] == jnp.arange(INNER, dtype=jnp.int32)[:, None]).astype(F32)
    return jnp.einsum("qcg,hg->qch", left, right, precision=lax.Precision.HIGHEST)


VMEM = pl.BlockSpec(memory_space=pltpu.VMEM)


def call_kernel(body, name, *inputs, outs, scratch=(), limit=16, call=pl.pallas_call):
    return call(
        body,
        out_shape=outs,
        in_specs=[VMEM] * len(inputs),
        out_specs=jax.tree.map(lambda _: VMEM, outs),
        scratch_shapes=scratch,
        compiler_params=pltpu.CompilerParams(vmem_limit_bytes=limit << 20),
        name=name,
    )(*inputs)


def local_blocks(data, slab, weight, call=pl.pallas_call):
    return call_kernel(
        block_kernel,
        "pair_blocks",
        data,
        slab,
        weight,
        *constants(),
        outs=(
            jax.ShapeDtypeStruct((128, 128), F32),
            jax.ShapeDtypeStruct((16, 4, 128), F32),
        ),
        scratch=[
            pltpu.VMEM((OUTER, 48, INNER), F32),
            pltpu.VMEM((GROUPS, 256, 2 * INNER), F32),
            pltpu.VMEM((2, 2, 128, 512), BF),
            pltpu.VMEM((2, 2, 128, 512), BF),
            pltpu.VMEM((2, 128, 128), F32),
        ],
        limit=32,
        call=call,
    )


def shards(waves, screen, pair_table, plane_map, trial, probe):
    n_rows = lax.axis_size("ka")
    n_cols = lax.axis_size("kp")
    own = waves.reshape(32, INNER)
    probe_rows = probe.reshape(2, 8, 8, 4).transpose(3, 0, 2, 1).reshape(4, 128)
    probe_rows = jnp.concatenate([probe_rows, jnp.zeros((4, 128), BF)], axis=0)

    out = call_kernel(
        first_kernel,
        "first",
        own,
        trial.reshape(64, 8).T,
        outs=jax.ShapeDtypeStruct((n_rows, SLAB, 128), BF),
    )
    slab = lax.all_to_all(out, "ka", 0, 0, tiled=True)
    out = call_kernel(
        second_kernel,
        "second",
        own,
        probe_rows,
        slab,
        outs=jax.ShapeDtypeStruct((n_cols, BLOCK, 128), BF),
    )
    data = lax.all_to_all(out, "kp", 0, 0, tiled=True)

    weight = make_weight(screen, pair_table, plane_map, plane_map.shape[0], OUTER * INNER)
    applied, adjoint = local_blocks(data, slab, weight)

    applied = lax.all_to_all(applied.reshape(n_cols, 4, 128), "kp", 0, 0, tiled=True)
    adjoint = lax.all_to_all(adjoint, "ka", 0, 0, tiled=True)
    applied = applied.sum(axis=0)
    applied = applied.reshape(4, 2, 8, 8).transpose(1, 3, 2, 0).reshape(2, 64, 4)
    adjoint = call_kernel(
        last_kernel, "last", adjoint, outs=jax.ShapeDtypeStruct((8, 64), F32)
    )
    return applied, adjoint.T.reshape(1, 64, 8)


def solution(mesh):
    placed = (
        P("ka", None, "kp"),
        P(),
        P("ka", "kp"),
        P(),
        P("kp", None, "ka"),
        P("ka", None, "kp"),
    )
    return jax.shard_map(
        shards,
        mesh=mesh,
        in_specs=placed,
        out_specs=(P("ka", None, "kp"), P("kp", None, "ka")),
        check_vma=False,
    )
```

time: 107 us -> 101 us (0.944)
  Pallas kernels: 11.5 us -> 8.85 us
  local copies, waits for them, and re-layouts: 6.21 us -> 3.75 us
    pallas_call x1 -> x4, Pallas kernels: 11.5 us -> 8.85 us  [call_kernel(): call(body, out_shape=outs, in_specs=[VMEM] * len(inputs), out_specs=jax.t...]
    transpose x3 -> x0, local copies, waits for them, and re-layouts: 1.41 us -> none  [the longest x1 0.72 us: shards(): trial_rows = trial.reshape(64, 2, 4).transpose(2, 1, 0).reshape(4, 128)]
  transfers between devices with their start and end apart: 3 -> 3, of which waited for: 3 -> 3; matrix products, arithmetic and copies ran while one was open for 2% -> 1% of each run, Pallas kernels for 0% -> 1%
where the time goes in v2:
time: 101 us; the launch traced here: 100 us
  starting transfers between devices  35.2 us (35%)
  waiting for transfers between devices  34.3 us (34%)
  blocking collectives  16.5 us (16%)
  Pallas kernels  8.85 us (9%)
  local copies, waits for them, and re-layouts  3.75 us (4%)
    all_to_all x1, starting transfers between devices, shards(): slab = lax.all_to_all(out, 'ka', 0, 0, tiled=True)  18.3 us
    all_to_all x1, blocking collectives, shards(): adjoint = lax.all_to_all(adjoint, 'ka', 0, 0, tiled=True)  16.5 us
    all_to_all x1, waiting for transfers between devices, shards(): data = lax.all_to_all(out, 'kp', 0, 0, tiled=True)  13.8 us
    all_to_all x1, waiting for transfers between devices, shards(): slab = lax.all_to_all(out, 'ka', 0, 0, tiled=True)  13.5 us
    all_to_all x1, starting transfers between devices, shards(): data = lax.all_to_all(out, 'kp', 0, 0, tiled=True)  11.4 us
    pallas_call x4, Pallas kernels, call_kernel(): call(body, out_shape=outs, in_specs=[VMEM] * len(inputs), out_specs=jax.t...  8.85 us
    all_to_all x1, waiting for transfers between devices, shards(): lax.all_to_all(applied.reshape(n_cols, 4, 128), 'kp', 0, 0, tiled=True)  7.06 us
    all_to_all x1, starting transfers between devices, shards(): lax.all_to_all(applied.reshape(n_cols, 4, 128), 'kp', 0, 0, tiled=True)  5.43 us
  transfers between devices with their start and end apart: 3, of which 3 were waited for; matrix products, arithmetic and copies ran while one was open for 1% of the time, Pallas kernels for 1%

profile of v2, /device:TPU:1, one launch (start us, length us, event | category | flops | bytes accessed | tf_op | source)
XLA Modules:
  0.0 100.1 jit_solution(4855411946440961912)
XLA Ops:
  0.7 0.7 copy-done.5
  1.4 0.7 copy-done.3
  2.1 0.7 first.1
  2.7 18.3 %all-to-all-start = ((bf16[16,40,128]{2,1,0:T(8,128)(2,1)}), bf16[16,40,128]{2,1,0:T(8,128)(2,1)S(1)}, u32[]{:S(2)}, u32[]{:S(2)}) async-start(bf16[16,40,128]{2,1,0:T(8,128)(2,1)} %first.1), calls=%async_computation | async-start | bytes 327680 | tf_op jit(solution)/shard_map/all_to_all | solution.py:260
  21.1 0.1 reshape.87
  21.2 0.1 copy.12
  21.3 0.1 reshape.88
  21.4 0.6 copy-done.8
  22.0 13.5 %all-to-all-done.slab = bf16[16,40,128]{2,1,0:T(8,128)(2,1)S(1)} async-done(((bf16[16,40,128]{2,1,0:T(8,128)(2,1)}), bf16[16,40,128]{2,1,0:T(8,128)(2,1)S(1)}, u32[]{:S(2)}, u32[]{:S(2)}) %all-to-all-start) | async-done | bytes 163872 | tf_op jit(solution)/shard_map/all_to_all | solution.py:260
  35.5 0.8 second.1
  36.3 11.4 %all-to-all-start.1 = ((bf16[32,56,128]{2,1,0:T(8,128)(2,1)}), bf16[32,56,128]{2,1,0:T(8,128)(2,1)S(1)}, u32[]{:S(2)}, u32[]{:S(2)}) async-start(bf16[32,56,128]{2,1,0:T(8,128)(2,1)} %second.1), calls=%async_computation.1 | async-start | bytes 917504 | tf_op jit(solution)/shard_map/all_to_all | solution.py:269
  47.8 0.6 gather_fusion
  48.4 0.1 select_multiply_fusion
  48.5 0.1 iota_compare_fusion.2
  48.6 0.4 fusion.1.weight
  49.0 13.8 %all-to-all-done.1.data = bf16[32,56,128]{2,1,0:T(8,128)(2,1)S(1)} async-done(((bf16[32,56,128]{2,1,0:T(8,128)(2,1)}), bf16[32,56,128]{2,1,0:T(8,128)(2,1)S(1)}, u32[]{:S(2)}, u32[]{:S(2)}) %all-to-all-start.1) | async-done | bytes 458784 | tf_op jit(solution)/shard_map/all_to_all | solution.py:269
  62.8 6.7 %pair_blocks.1 = (f32[128,128]{1,0:T(8,128)}, f32[16,4,128]{2,1,0:T(4,128)S(1)}) custom-call(bf16[32,56,128]{2,1,0:T(8,128)(2,1)S(1)} %all-to-all-done.1.data, bf16[16,40,128]{2,1,0:T(8,128)(2,1)S(1)} %all-to-all-done.slab, f32[2,17,128]{2,1,0:T(8,128)S(1)} %fusion.1.weight, bf16[768,256]{1,0:T(8,128)(2,1)S(1)} %copy-done.1, f32[34,8,128]{2,1,0:T(8,128)S(1)} %copy-done.2), custom_call_target="tpu_custom_call" | custom-call | tf_op jit(solution)/shard_map/pair_blocks/pallas_call | solution.py:211
  69.5 16.5 %all_to_all.20.parts = f32[16,4,128]{2,1,0:T(4,128)S(1)} all-to-all(f32[16,4,128]{2,1,0:T(4,128)S(1)} %get-tuple-element.5), channel_id=1, replica_groups=mesh['ka'=16,'kp'=32] {'ka'}, dimensions={0} | all-to-all | bytes 65536 | tf_op jit(solution)/shard_map/all_to_all | solution.py:275
  86.0 5.4 %all-to-all-start.2 = ((f32[32,4,128]{2,1,0:T(4,128)}), f32[32,4,128]{2,1,0:T(4,128)S(1)}, u32[]{:S(2)}, u32[]{:S(2)}) async-start(f32[32,4,128]{2,1,0:T(4,128)} %bitcast.7), calls=%async_computation.2 | async-start | bytes 131072 | tf_op jit(solution)/shard_map/all_to_all | solution.py:274
  91.4 0.7 last.1
  92.1 7.1 %all-to-all-done.2 = f32[32,4,128]{2,1,0:T(4,128)S(1)} async-done(((f32[32,4,128]{2,1,0:T(4,128)}), f32[32,4,128]{2,1,0:T(4,128)S(1)}, u32[]{:S(2)}, u32[]{:S(2)}) %all-to-all-start.2) | async-done | bytes 65568 | tf_op jit(solution)/shard_map/all_to_all | solution.py:274
  99.2 0.1 reshape.91
  99.3 0.1 copy.13
  99.4 0.7 reshape.92
  (26 shorter events, 0.2 us)
Async XLA Ops:
  0.6 47.1 %copy-start = (f32[32,512]{1,0:T(8,128)S(1)}, f32[32,512]{1,0:T(8,128)}, u32[]{:S(2)}) copy-start(f32[32,512]{1,0:T(8,128)} %param.9) | copy-start | bytes 196612
  0.6 0.7 copy-start.5
  1.4 0.7 copy-start.3
  2.7 18.3 %copy-start.6 = (bf16[2,64,4]{1,2,0:T(4,128)(2,1)S(1)}, bf16[2,64,4]{1,2,0:T(4,128)(2,1)}, u32[]{:S(2)}) copy-start(bf16[2,64,4]{1,2,0:T(4,128)(2,1)} %param.13) | copy-start | bytes 3076
  2.7 32.7 %all-to-all-start = ((bf16[16,40,128]{2,1,0:T(8,128)(2,1)}), bf16[16,40,128]{2,1,0:T(8,128)(2,1)S(1)}, u32[]{:S(2)}, u32[]{:S(2)}) async-start(bf16[16,40,128]{2,1,0:T(8,128)(2,1)} %first.1), calls=%async_computation | async-start | bytes 327680 | tf_op jit(solution)/shard_map/all_to_all | solution.py:260
  21.3 14.2 %copy-start.4 = (bf16[2,16,128]{2,1,0:T(8,128)(2,1)S(1)}, bf16[2,16,128]{2,1,0:T(8,128)(2,1)}, u32[]{:S(2)}) copy-start(bf16[2,16,128]{2,1,0:T(8,128)(2,1)} %param.8) | copy-start | bytes 24580
  21.4 0.7 copy-start.8
  36.3 12.1 %copy-start.7 = (s32[512]{0:T(512)S(1)}, s32[512]{0:T(512)}, u32[]{:S(2)}) copy-start(s32[512]{0:T(512)} %param.11) | copy-start | bytes 6148
  36.3 26.5 %copy-start.2 = (f32[34,8,128]{2,1,0:T(8,128)S(1)}, f32[34,8,128]{2,1,0:T(8,128)}, u32[]{:S(2)}) copy-start(f32[34,8,128]{2,1,0:T(8,128)} %constant.69.clone.table) | copy-start | bytes 417796
  36.3 26.5 %all-to-all-start.1 = ((bf16[32,56,128]{2,1,0:T(8,128)(2,1)}), bf16[32,56,128]{2,1,0:T(8,128)(2,1)S(1)}, u32[]{:S(2)}, u32[]{:S(2)}) async-start(bf16[32,56,128]{2,1,0:T(8,128)(2,1)} %second.1), calls=%async_computation.1 | async-start | bytes 917504 | tf_op jit(solution)/shard_map/all_to_all | solution.py:269
  47.8 15.1 %copy-start.1 = (bf16[768,256]{1,0:T(8,128)(2,1)S(1)}, bf16[768,256]{1,0:T(8,128)(2,1)}, u32[]{:S(2)}) copy-start(bf16[768,256]{1,0:T(8,128)(2,1)} %constant.68.clone.matrix) | copy-start | bytes 1179652
  86.0 13.2 %all-to-all-start.2 = ((f32[32,4,128]{2,1,0:T(4,128)}), f32[32,4,128]{2,1,0:T(4,128)S(1)}, u32[]{:S(2)}, u32[]{:S(2)}) async-start(f32[32,4,128]{2,1,0:T(4,128)} %bitcast.7), calls=%async_computation.2 | async-start | bytes 131072 | tf_op jit(solution)/shard_map/all_to_all | solution.py:274

commit v3 on v2

v3 whole, which is shorter than its diff:
```python
import math

import jax
import jax.numpy as jnp
import numpy as np
from jax import lax
from jax.experimental import pallas as pl
from jax.experimental.pallas import tpu as pltpu
from jax.sharding import PartitionSpec as P

NV = 8
NC = 8
OUTER = 32
INNER = 128
BLOCK = 56
SLAB = 48
GROUPS = OUTER // 2 + 1
UNROLL = 4
BF = jnp.bfloat16
F32 = jnp.float32


def split_np(values):
    high = np.asarray(values, np.float32).astype(jnp.bfloat16)
    low = (np.asarray(values, np.float64) - high.astype(np.float64)).astype(jnp.bfloat16)
    return high, low


def constants():
    inner = np.arange(INNER)
    angle = 2.0 * np.pi * ((inner[:, None] * inner[None, :]) % INNER) / INNER
    cos, sin = np.cos(angle), np.sin(angle)
    high, low = split_np(np.block([[cos, -sin], [sin, cos]]))
    group = np.arange(GROUPS)
    twist = 2.0 * np.pi * (group[:, None] * inner[None, :]) / (OUTER * INNER)
    table = np.stack([np.cos(twist), np.sin(twist)], axis=1).reshape(2 * GROUPS, 1, INNER)
    table = np.broadcast_to(table, (2 * GROUPS, 8, INNER)).astype(np.float32)
    order = np.zeros((2, 128, 128), np.float32)
    for spot in range(64):
        for side in range(2):
            order[side, side * 64 + spot, spot % 8 * 8 + spot // 8] = 1.0
    return (
        np.concatenate([high, high, low], axis=0),
        np.ascontiguousarray(table),
        order.astype(jnp.bfloat16),
    )


def real_fft(x):
    n = len(x)
    if n == 2:
        return [x[0] + x[1], x[0] - x[1]], [None, None]
    even_re, even_im = real_fft(x[0::2])
    odd_re, odd_im = real_fft(x[1::2])
    half = n // 2
    out_re, out_im = [None] * (half + 1), [None] * (half + 1)
    out_re[0] = even_re[0] + odd_re[0]
    out_re[half] = even_re[0] - odd_re[0]
    out_re[half // 2] = even_re[half // 2]
    out_im[half // 2] = -odd_re[half // 2]
    for k in range(1, half // 2):
        c, s = math.cos(2 * math.pi * k / n), math.sin(2 * math.pi * k / n)
        if 8 * k == n:
            turn_re = (odd_re[k] + odd_im[k]) * c
            turn_im = (odd_im[k] - odd_re[k]) * c
        else:
            turn_re = odd_re[k] * c + odd_im[k] * s
            turn_im = odd_im[k] * c - odd_re[k] * s
        out_re[k] = even_re[k] + turn_re
        out_im[k] = even_im[k] + turn_im
        out_re[half - k] = even_re[k] - turn_re
        out_im[half - k] = turn_im - even_im[k]
    return out_re, out_im


def split(x):
    high = x.astype(BF)
    return high, (x - high.astype(F32)).astype(BF)


def dot(a, b):
    return lax.dot_general(a, b, (((1,), (0,)), ((), ())), preferred_element_type=F32)


def dot_t(a, b):
    return lax.dot_general(a, b, (((1,), (1,)), ((), ())), preferred_element_type=F32)


def first_kernel(pair, own, trial, probe, out, pair_here, own_here, trial_here, probe_here, sems):
    copies = [
        pltpu.make_async_copy(source, target, sems.at[i])
        for i, (source, target) in enumerate(
            ((pair, pair_here), (own, own_here), (trial, trial_here), (probe, probe_here))
        )
    ]
    for copy in copies:
        copy.start()
    for copy in copies:
        copy.wait()
    side = jnp.concatenate([trial_here[...], probe_here[...]], axis=1)
    spot = lax.broadcasted_iota(jnp.int32, (8, 128), 0)
    index = jnp.where(spot == 0, pair_here[0], pair_here[1]).astype(F32).astype(BF)
    for i in range(out.shape[0]):
        out[i, :32, :] = own_here[...]
        out[i, 32:40, :] = side
        out[i, 40:, :] = index


def second_kernel(own, slab, out):
    for i in range(out.shape[0]):
        half = i % 2
        out[i, :32, :] = own[...]
        out[i, 32:48, :] = slab[i // 2, half * 16 : half * 16 + 16, :]
        rest = slab[i // 2, 32:48, :].astype(F32)
        index = jnp.broadcast_to(rest[8 + half : 9 + half], (4, 128))
        rest = jnp.concatenate([rest[half * 4 : half * 4 + 4], index], axis=0)
        out[i, 48:, :] = rest.astype(BF)


def last_kernel(parts, applied, adjoint):
    total = parts[...].sum(axis=0)
    applied[0] = total[:4, :64]
    applied[1] = total[:4, 64:]
    adjoint[:4, :] = total[4:, :64]
    adjoint[4:, :] = total[4:, 64:]


def blocks_moved(both):
    spot = lax.broadcasted_iota(jnp.int32, (8, 128), 1) // 8 % 8
    rows = []
    for new in range(8):
        row = jnp.zeros((8, 128), F32)
        for old in range(8):
            block = both[old * 8 : old * 8 + 8]
            shift = (old - new) * 8 % 128
            if shift:
                block = pltpu.roll(block, shift, 1)
            row = jnp.where(spot == old, block, row)
        rows.append(row)
    moved = jnp.concatenate(rows, axis=0)
    return jnp.concatenate([moved, pltpu.roll(moved, 64, 1)], axis=0)


def block_kernel(
    pair, place, data, slab, screens, matrix, table, order, out, wide, grid, val, con, acc, weight
):
    wide[...] = data[:, :48, :].astype(F32)
    for q in range(2):
        weight[q] = screens[pair[q]]
        other = data[pl.ds(2 * place[0] + q, 1), 52:56, :].astype(F32)
        weight[2 + q] = screens[jnp.max(other).astype(jnp.int32)]

    def transform(i):
        q, t, s = i // 16, i // 8 % 2, i % 8
        single = (1 - t) * (q * 16) + t * 40 + s
        side = pl.multiple_of((1 - t) * 32 + t * (q * 16 + 8), 8)
        base = pl.multiple_of(i * 8, 8)
        tiles = [
            jnp.broadcast_to(wide[a, pl.ds(single, 1), :], (8, INNER)) * wide[a, pl.ds(side, 8), :]
            for a in range(OUTER)
        ]
        re, im = real_fft(tiles)
        for c in range(GROUPS):
            if c == 0:
                new_re, new_im = re[0], jnp.zeros_like(re[0])
            elif c == GROUPS - 1:
                new_re, new_im = re[c] * table[2 * c], -(re[c] * table[2 * c + 1])
            else:
                cos, sin = table[2 * c], table[2 * c + 1]
                new_re = re[c] * cos + im[c] * sin
                new_im = im[c] * cos - re[c] * sin
            grid[c, pl.ds(base, 8), :INNER] = new_re
            grid[c, pl.ds(base, 8), INNER:] = new_im

    def transform_some(i, carry):
        for part in range(UNROLL):
            transform(i * UNROLL + part)
        return carry

    lax.fori_loop(0, 32 // UNROLL, transform_some, 0)
    acc[...] = jnp.zeros_like(acc)

    def spectra(c, count, slot):
        x = grid[pl.ds(c, count)].reshape(count * 256, 256)
        x_high, x_low = split(x)
        s = dot(jnp.concatenate([x_high, x_low, x_high], axis=1), matrix[...])
        for part in range(count):
            lanes = slice(part * 256, part * 256 + 256)
            for q in range(2):
                row = part * 256 + q * 128
                val[slot, q, :, lanes] = jnp.concatenate(split(s[row : row + 64]), axis=0)
                for side in range(2):
                    w = weight[2 * side + q, pl.ds(c + part, 1), :]
                    w = jnp.concatenate([w, w], axis=1)
                    rows = slice(side * 128, side * 128 + 128)
                    con[slot, q, rows, lanes] = jnp.concatenate(
                        split(s[row + 64 : row + 128] * w), axis=0
                    )

    def contract(slot):
        for q in range(2):
            acc[q] += dot_t(con[slot, q], val[slot, q])

    def four_groups(t, carry):
        spectra(4 * t + 1, 2, 1)
        contract(0)
        spectra(4 * t + 3, 2, 0)
        contract(1)
        return carry

    val[0, :, :, 256:] = jnp.zeros((2, 128, 256), BF)
    con[0, :, :, 256:] = jnp.zeros((2, 256, 256), BF)
    spectra(0, 1, 0)
    lax.fori_loop(0, GROUPS // 4, four_groups, 0)
    contract(0)

    inputs = (slab[:, 32:40, :].astype(F32).reshape(128, 128), data[:, 48:52, :].reshape(128, 128))
    lane = lax.broadcasted_iota(jnp.int32, (64, 128), 1)
    results = []
    for side in range(2):
        twice = []
        for q in range(2):
            part = acc[q, side * 128 : side * 128 + 64, :]
            part = part + acc[q, side * 128 + 64 : side * 128 + 128, :]
            twice.append(part + pltpu.roll(part, 64, 1))
        high, low = split(blocks_moved(jnp.where(lane < 64, twice[0], twice[1])))
        columns = dot(inputs[side].astype(BF), order[side]).astype(BF)
        results.append(dot_t(columns, high) + dot_t(columns, low))

    first, full = results
    lane = lax.broadcasted_iota(jnp.int32, (128, 128), 1)
    spot = lax.broadcasted_iota(jnp.int32, (128, 128), 0) % 8
    down = pltpu.roll(full, 4, 0)
    even = jnp.where(lane < 64, down, pltpu.roll(full, 64, 1))
    odd = jnp.where(lane < 64, pltpu.roll(down, 64, 1), full)
    even = jnp.where(spot < 4, first, even)
    odd = jnp.where(spot < 4, pltpu.roll(first, 124, 0), odd)
    out[:, 0] = even.reshape(16, 8, 128)
    out[:, 1] = odd.reshape(16, 8, 128)


def make_weight(screen, plane_map, planes, points):
    chosen = screen * (1.0 / (planes * points))
    group = jnp.arange(GROUPS, dtype=jnp.int32)[:, None]
    other = points - plane_map
    direct = (plane_map % OUTER)[None, :] == group
    mirror = ((other % OUTER)[None, :] == group) & (group > 0) & (group < GROUPS - 1)
    mask = jnp.concatenate([direct, mirror], axis=1).astype(F32)
    left = mask[None] * jnp.concatenate([chosen, chosen], axis=1)[:, None, :]
    spot = jnp.concatenate([plane_map // OUTER, other // OUTER])
    right = (spot[None, :] == jnp.arange(INNER, dtype=jnp.int32)[:, None]).astype(F32)
    return jnp.einsum("qcg,hg->qch", left, right, precision=lax.Precision.HIGHEST)


VMEM = pl.BlockSpec(memory_space=pltpu.VMEM)
SMEM = pl.BlockSpec(memory_space=pltpu.SMEM)


def call_kernel(
    body, name, *inputs, outs, scalars=0, space=VMEM, scratch=(), limit=16, call=pl.pallas_call
):
    return call(
        body,
        out_shape=outs,
        in_specs=[SMEM] * scalars + [space] * (len(inputs) - scalars),
        out_specs=jax.tree.map(lambda _: VMEM, outs),
        scratch_shapes=scratch,
        compiler_params=pltpu.CompilerParams(vmem_limit_bytes=limit << 20),
        name=name,
    )(*inputs)


def local_blocks(pair, place, data, slab, screens, call=pl.pallas_call):
    return call_kernel(
        block_kernel,
        "pair_blocks",
        pair,
        place,
        data,
        slab,
        screens,
        *constants(),
        scalars=2,
        outs=jax.ShapeDtypeStruct((16, 2, 8, 128), F32),
        scratch=[
            pltpu.VMEM((OUTER, 48, INNER), F32),
            pltpu.VMEM((GROUPS, 256, 2 * INNER), F32),
            pltpu.VMEM((2, 2, 128, 512), BF),
            pltpu.VMEM((2, 2, 256, 512), BF),
            pltpu.VMEM((2, 256, 128), F32),
            pltpu.VMEM((4, GROUPS, INNER), F32),
        ],
        limit=32,
        call=call,
    )


def shards(waves, screen, pair_table, plane_map, trial, probe):
    n_rows = lax.axis_size("ka")
    n_cols = lax.axis_size("kp")
    own = waves.reshape(32, INNER)
    pair = pair_table.reshape(2)
    place = lax.axis_index("ka").astype(jnp.int32).reshape(1)

    stay = (pair, own, trial.reshape(64, 8).T, probe.transpose(0, 2, 1).reshape(8, 64))
    stay = [pltpu.with_memory_space_constraint(x, pltpu.HBM) for x in stay]
    out = call_kernel(
        first_kernel,
        "first",
        *stay,
        space=pl.BlockSpec(memory_space=pltpu.HBM),
        outs=jax.ShapeDtypeStruct((n_rows, SLAB, 128), BF),
        scratch=[
            pltpu.SMEM((2,), jnp.int32),
            pltpu.VMEM((32, 128), BF),
            pltpu.VMEM((8, 64), BF),
            pltpu.VMEM((8, 64), BF),
            pltpu.SemaphoreType.DMA((4,)),
        ],
    )
    slab = lax.all_to_all(out, "ka", 0, 0, tiled=True)
    out = call_kernel(
        second_kernel, "second", own, slab, outs=jax.ShapeDtypeStruct((n_cols, BLOCK, 128), BF)
    )
    data = lax.all_to_all(out, "kp", 0, 0, tiled=True)

    screens = make_weight(screen, plane_map, plane_map.shape[0], OUTER * INNER)
    out = local_blocks(pair, place, data, slab, screens)

    parts = lax.all_to_all(out.reshape(n_cols, 8, 128), "kp", 0, 0, tiled=True)
    applied, adjoint = call_kernel(
        last_kernel,
        "last",
        parts,
        outs=(jax.ShapeDtypeStruct((2, 4, 64), F32), jax.ShapeDtypeStruct((8, 64), F32)),
    )
    swap = [
        (a * n_cols + 2 * b + c, b * n_cols + 2 * a + c)
        for a in range(n_rows)
        for b in range(n_rows)
        for c in range(2)
    ]
    adjoint = lax.ppermute(adjoint, ("ka", "kp"), swap)
    return applied.transpose(0, 2, 1), adjoint.T.reshape(1, 64, 8)


def solution(mesh):
    placed = (
        P("ka", None, "kp"),
        P(),
        P("ka", "kp"),
        P(),
        P("kp", None, "ka"),
        P("ka", None, "kp"),
    )
    return jax.shard_map(
        shards,
        mesh=mesh,
        in_specs=placed,
        out_specs=(P("ka", None, "kp"), P("kp", None, "ka")),
        check_vma=False,
    )
```

time: 101 us -> 96.1 us (0.951)
  the two profiles are of different devices: /device:TPU:1 before, /device:TPU:68 now
where the time goes in v3:
time: 96.1 us; the launch traced here: 95.8 us
  blocking collectives  47.1 us (49%)
  waiting for transfers between devices  24 us (25%)
  starting transfers between devices  12 us (12%)
  Pallas kernels  9.68 us (10%)
  matrix products  1.24 us (1%)
    all_to_all x1, blocking collectives, shards(): slab = lax.all_to_all(out, 'ka', 0, 0, tiled=True)  34.9 us
    ppermute x1, waiting for transfers between devices, shards(): adjoint = lax.ppermute(adjoint, ('ka', 'kp'), swap)  12.3 us
    all_to_all x1, blocking collectives, shards(): parts = lax.all_to_all(out.reshape(n_cols, 8, 128), 'kp', 0, 0, tiled=True)  12.2 us
    all_to_all x1, waiting for transfers between devices, shards(): data = lax.all_to_all(out, 'kp', 0, 0, tiled=True)  11.7 us
    pallas_call x4, Pallas kernels, call_kernel(): call(body, out_shape=outs, in_specs=[SMEM] * scalars + [space] * (len(inp...  9.68 us
    all_to_all x1, starting transfers between devices, shards(): data = lax.all_to_all(out, 'kp', 0, 0, tiled=True)  7.13 us
    ppermute x1, starting transfers between devices, shards(): adjoint = lax.ppermute(adjoint, ('ka', 'kp'), swap)  4.86 us
  transfers between devices with their start and end apart: 2, of which 2 were waited for; matrix products, arithmetic and copies ran while one was open for 2% of the time, Pallas kernels for 0%

profile of v3, /device:TPU:68, one launch (start us, length us, event | category | flops | bytes accessed | tf_op | source)
XLA Modules:
  0.0 95.8 jit_solution(17133538491562659160)
XLA Ops:
  0.6 0.0 copy-start.3
  0.6 0.9 first.1
  1.6 34.9 %all_to_all.15.slab = bf16[16,48,128]{2,1,0:T(8,128)(2,1)S(1)} all-to-all(bf16[16,48,128]{2,1,0:T(8,128)(2,1)S(1)} %first.1), channel_id=1, replica_groups=mesh['ka'=16,'kp'=32] {'ka'}, dimensions={0} | all-to-all | bytes 393216 | tf_op jit(solution)/shard_map/all_to_all | solution.py:321
  36.4 0.0 copy-done.3
  36.4 0.8 second.1
  37.3 7.1 %all-to-all-start.1 = ((bf16[32,56,128]{2,1,0:T(8,128)(2,1)}), bf16[32,56,128]{2,1,0:T(8,128)(2,1)S(1)}, u32[]{:S(2)}, u32[]{:S(2)}) async-start(bf16[32,56,128]{2,1,0:T(8,128)(2,1)} %second.1), calls=%async_computation.1 | async-start | bytes 917504 | tf_op jit(solution)/shard_map/all_to_all | solution.py:325
  44.5 0.0 copy-done.6
  44.5 0.1 iota_compare_fusion.2
  44.6 0.0 copy-done.5
  44.6 1.2 %fusion = f32[32,17,128]{2,0,1:T(8,128)S(1)} fusion(f32[32,1024]{1,0:T(8,128)S(1)} %pad_maximum_fusion, f32[17,1024]{1,0:T(8,128)S(1)} %add_convert_fusion, s32[1024]{0:T(1024)S(1)} %pad_add_fusion), kind=kOutput, calls=%fused_computation | convolution fusion | flops 856326144 | bytes 483328 | tf_op jit(solution)/shard_map/qcg,hg->qch/dot_general | solution.py:252
  45.9 0.0 copy-start
  45.9 0.0 copy-start.1
  45.9 0.0 copy-start.2
  45.9 0.0 copy-start.4
  45.9 0.2 copy.11.screens
  46.1 11.7 %all-to-all-done.1.data = bf16[32,56,128]{2,1,0:T(8,128)(2,1)S(1)} async-done(((bf16[32,56,128]{2,1,0:T(8,128)(2,1)}), bf16[32,56,128]{2,1,0:T(8,128)(2,1)S(1)}, u32[]{:S(2)}, u32[]{:S(2)}) %all-to-all-start.1) | async-done | bytes 458784 | tf_op jit(solution)/shard_map/all_to_all | solution.py:325
  57.8 0.0 copy-done.2
  57.8 0.0 copy-done.4
  57.8 7.2 %pair_blocks.1 = f32[16,2,8,128]{3,2,1,0:T(8,128)S(1)} custom-call(s32[2]{0:T(128)S(1)} %bitcast.21, s32[1]{0:T(128)} %bitcast.1.place, bf16[32,56,128]{2,1,0:T(8,128)(2,1)S(1)} %all-to-all-done.1.data, bf16[16,48,128]{2,1,0:T(8,128)(2,1)S(1)} %all_to_all.15.slab, f32[32,17,128]{2,1,0:T(8,128)S(1)} %copy.11.screens, bf16[768,256]{1,0:T(8,128)(2,1)S(1)} %copy-done, ...), custom_call_target="tpu_custom_call" | custom-call | tf_op jit(solution)/shard_map/pair_blocks/pallas_call | solution.py:262
  65.1 12.2 %all_to_all.16.parts = f32[32,8,128]{2,1,0:T(8,128)S(1)} all-to-all(f32[32,8,128]{2,1,0:T(8,128)S(1)} %bitcast.17), channel_id=1, replica_groups=mesh['ka'=16,'kp'=32] {'kp'}, dimensions={0} | all-to-all | bytes 262144 | tf_op jit(solution)/shard_map/all_to_all | solution.py:330
  77.3 0.7 last.1
  78.0 4.9 %collective-permute-start = (f32[8,64]{1,0:T(8,128)S(1)}, f32[8,64]{1,0:T(8,128)S(1)}, u32[]{:S(2)}, u32[]{:S(2)}) collective-permute-start(f32[8,64]{1,0:T(8,128)S(1)} %get-tuple-element.5), channel_id=1, source_target_pairs={{0,0},{1,1},{2,32},{3,33},{4,64},{5,65},{6,96},{7,97},{8,128},{9,1... | collective-permute-start | bytes 6152 | tf_op jit(solution)/shard_map/ppermute | solution.py:343
  82.9 12.3 %collective-permute-done = f32[8,64]{1,0:T(8,128)S(1)} collective-permute-done((f32[8,64]{1,0:T(8,128)S(1)}, f32[8,64]{1,0:T(8,128)S(1)}, u32[]{:S(2)}, u32[]{:S(2)}) %collective-permute-start) | collective-permute-done | bytes 2080 | tf_op jit(solution)/shard_map/ppermute | solution.py:343
  95.2 0.6 copy.13
  (11 shorter events, 0.1 us)
Async XLA Ops:
  0.6 35.8 %copy-start.3 = (bf16[2,16,128]{2,1,0:T(8,128)(2,1)S(1)}, bf16[2,16,128]{2,1,0:T(8,128)(2,1)}, u32[]{:S(2)}) copy-start(bf16[2,16,128]{2,1,0:T(8,128)(2,1)} %param.9) | copy-start | bytes 24580
  37.3 7.2 %copy-start.6 = (s32[512]{0:T(512)S(1)}, s32[512]{0:T(512)}, u32[]{:S(2)}) copy-start(s32[512]{0:T(512)} %param.12) | copy-start | bytes 6148
  37.3 7.3 %copy-start.5 = (f32[32,512]{1,0:T(8,128)S(1)}, f32[32,512]{1,0:T(8,128)}, u32[]{:S(2)}) copy-start(f32[32,512]{1,0:T(8,128)} %param.10) | copy-start | bytes 196612
  37.3 20.5 %all-to-all-start.1 = ((bf16[32,56,128]{2,1,0:T(8,128)(2,1)}), bf16[32,56,128]{2,1,0:T(8,128)(2,1)S(1)}, u32[]{:S(2)}, u32[]{:S(2)}) async-start(bf16[32,56,128]{2,1,0:T(8,128)(2,1)} %second.1), calls=%async_computation.1 | async-start | bytes 917504 | tf_op jit(solution)/shard_map/all_to_all | solution.py:325
  45.9 11.9 %copy-start = (bf16[768,256]{1,0:T(8,128)(2,1)S(1)}, bf16[768,256]{1,0:T(8,128)(2,1)}, u32[]{:S(2)}) copy-start(bf16[768,256]{1,0:T(8,128)(2,1)} %constant.59.clone.matrix) | copy-start | bytes 1179652
  45.9 11.9 %copy-start.1 = (f32[34,8,128]{2,1,0:T(8,128)S(1)}, f32[34,8,128]{2,1,0:T(8,128)}, u32[]{:S(2)}) copy-start(f32[34,8,128]{2,1,0:T(8,128)} %constant.60.clone.table) | copy-start | bytes 417796
  45.9 11.9 %copy-start.2 = (bf16[2,128,128]{2,1,0:T(8,128)(2,1)S(1)}, bf16[2,128,128]{2,1,0:T(8,128)(2,1)}, u32[]{:S(2)}) copy-start(bf16[2,128,128]{2,1,0:T(8,128)(2,1)} %constant.61.clone.order) | copy-start | bytes 196612
  45.9 11.9 %copy-start.4 = (s32[2,1]{0,1:T(1,128)S(1)}, s32[2,1]{0,1:T(1,128)}, u32[]{:S(2)}) copy-start(s32[2,1]{0,1:T(1,128)} %param.11) | copy-start | bytes 28
  78.0 17.2 %collective-permute-start = (f32[8,64]{1,0:T(8,128)S(1)}, f32[8,64]{1,0:T(8,128)S(1)}, u32[]{:S(2)}, u32[]{:S(2)}) collective-permute-start(f32[8,64]{1,0:T(8,128)S(1)} %get-tuple-element.5), channel_id=1, source_target_pairs={{0,0},{1,1},{2,32},{3,33},{4,64},{5,65},{6,96},{7,97},{8,128},{9,1... | collective-permute-start | bytes 6152 | tf_op jit(solution)/shard_map/ppermute | solution.py:343

commit v4 on v3

--- a/solution.py
+++ b/solution.py
@@ -16,6 +16,7 @@
 SLAB = 48
 GROUPS = OUTER // 2 + 1
 UNROLL = 4
+TURNS = (1, 0, 0, 3)
 BF = jnp.bfloat16
 F32 = jnp.float32
 
@@ -229,14 +230,18 @@
 
     first, full = results
     lane = lax.broadcasted_iota(jnp.int32, (128, 128), 1)
-    spot = lax.broadcasted_iota(jnp.int32, (128, 128), 0) % 8
     down = pltpu.roll(full, 4, 0)
     even = jnp.where(lane < 64, down, pltpu.roll(full, 64, 1))
     odd = jnp.where(lane < 64, pltpu.roll(down, 64, 1), full)
-    even = jnp.where(spot < 4, first, even)
-    odd = jnp.where(spot < 4, pltpu.roll(first, 124, 0), odd)
-    out[:, 0] = even.reshape(16, 8, 128)
-    out[:, 1] = odd.reshape(16, 8, 128)
+    first = first.reshape(16, 8, 128)
+    for i in range(32):
+        out[i // 8, i % 8, :4, :] = first[i // 2, i % 2 * 4 : i % 2 * 4 + 4, :]
+    zone = place[0] // 4
+    turn = jnp.where(zone == 0, TURNS[0], jnp.where(zone == 3, TURNS[3], 0))
+    for i in range(32):
+        spot = jnp.bitwise_and(i // 8 + turn, 3)
+        value = (even, odd)[i % 2][i // 2 * 8 + 4 : i // 2 * 8 + 8, :]
+        out[spot, (i // 2 + 2) % 4 * 2 + i % 2, 4:, :] = value
 
 
 def make_weight(screen, plane_map, planes, points):
@@ -281,7 +286,7 @@
         screens,
         *constants(),
         scalars=2,
-        outs=jax.ShapeDtypeStruct((16, 2, 8, 128), F32),
+        outs=jax.ShapeDtypeStruct((4, 8, 8, 128), F32),
         scratch=[
             pltpu.VMEM((OUTER, 48, INNER), F32),
             pltpu.VMEM((GROUPS, 256, 2 * INNER), F32),
@@ -334,12 +339,12 @@
         parts,
         outs=(jax.ShapeDtypeStruct((2, 4, 64), F32), jax.ShapeDtypeStruct((8, 64), F32)),
     )
-    swap = [
-        (a * n_cols + 2 * b + c, b * n_cols + 2 * a + c)
-        for a in range(n_rows)
-        for b in range(n_rows)
-        for c in range(2)
-    ]
+    swap = []
+    for a in range(n_rows):
+        for b in range(n_rows):
+            for c in range(2):
+                spot = (b // 4 + TURNS[a // 4]) % 4 * 8 + (b + 2) % 4 * 2 + c
+                swap.append((a * n_cols + spot, b * n_cols + 2 * a + c))
     adjoint = lax.ppermute(adjoint, ("ka", "kp"), swap)
     return applied.transpose(0, 2, 1), adjoint.T.reshape(1, 64, 8)
 

time: 96.1 us -> 95 us (0.989)
  the two profiles are of different devices: /device:TPU:68 before, /device:TPU:64 now
where the time goes in v4:
time: 95 us; the launch traced here: 94.7 us
  blocking collectives  48.4 us (51%)
  waiting for transfers between devices  23.3 us (25%)
  starting transfers between devices  10.3 us (11%)
  Pallas kernels  9.66 us (10%)
  matrix products  1.25 us (1%)
    all_to_all x1, blocking collectives, shards(): slab = lax.all_to_all(out, 'ka', 0, 0, tiled=True)  36.2 us
    all_to_all x1, blocking collectives, shards(): parts = lax.all_to_all(out.reshape(n_cols, 8, 128), 'kp', 0, 0, tiled=True)  12.2 us
    all_to_all x1, waiting for transfers between devices, shards(): data = lax.all_to_all(out, 'kp', 0, 0, tiled=True)  11.7 us
    ppermute x1, waiting for transfers between devices, shards(): adjoint = lax.ppermute(adjoint, ('ka', 'kp'), swap)  11.6 us
    pallas_call x4, Pallas kernels, call_kernel(): call(body, out_shape=outs, in_specs=[SMEM] * scalars + [space] * (len(inp...  9.66 us
    all_to_all x1, starting transfers between devices, shards(): data = lax.all_to_all(out, 'kp', 0, 0, tiled=True)  7.13 us
    ppermute x1, starting transfers between devices, shards(): adjoint = lax.ppermute(adjoint, ('ka', 'kp'), swap)  3.18 us
  transfers between devices with their start and end apart: 2, of which 2 were waited for; matrix products, arithmetic and copies ran while one was open for 2% of the time, Pallas kernels for 0%

profile of v4, /device:TPU:64, one launch (start us, length us, event | category | flops | bytes accessed | tf_op | source)
XLA Modules:
  0.0 94.7 jit_solution(12099206823730537311)
XLA Ops:
  0.6 0.0 copy-start.3
  0.6 0.9 first.1
  1.6 36.2 %all_to_all.15.slab = bf16[16,48,128]{2,1,0:T(8,128)(2,1)S(1)} all-to-all(bf16[16,48,128]{2,1,0:T(8,128)(2,1)S(1)} %first.1), channel_id=1, replica_groups=mesh['ka'=16,'kp'=32] {'ka'}, dimensions={0} | all-to-all | bytes 393216 | tf_op jit(solution)/shard_map/all_to_all | solution.py:326
  37.8 0.0 copy-done.3
  37.8 0.8 second.1
  38.6 7.1 %all-to-all-start.1 = ((bf16[32,56,128]{2,1,0:T(8,128)(2,1)}), bf16[32,56,128]{2,1,0:T(8,128)(2,1)S(1)}, u32[]{:S(2)}, u32[]{:S(2)}) async-start(bf16[32,56,128]{2,1,0:T(8,128)(2,1)} %second.1), calls=%async_computation.1 | async-start | bytes 917504 | tf_op jit(solution)/shard_map/all_to_all | solution.py:330
  45.8 0.0 copy-done.6
  45.8 0.1 iota_compare_fusion.2
  45.9 0.0 copy-done.5
  46.0 1.2 %fusion = f32[32,17,128]{2,0,1:T(8,128)S(1)} fusion(f32[32,1024]{1,0:T(8,128)S(1)} %pad_maximum_fusion, f32[17,1024]{1,0:T(8,128)S(1)} %add_convert_fusion, s32[1024]{0:T(1024)S(1)} %pad_add_fusion), kind=kOutput, calls=%fused_computation | convolution fusion | flops 856326144 | bytes 483328 | tf_op jit(solution)/shard_map/qcg,hg->qch/dot_general | solution.py:257
  47.2 0.0 copy-start
  47.2 0.0 copy-start.1
  47.2 0.0 copy-start.2
  47.2 0.0 copy-start.4
  47.3 0.2 copy.11.screens
  47.4 11.7 %all-to-all-done.1.data = bf16[32,56,128]{2,1,0:T(8,128)(2,1)S(1)} async-done(((bf16[32,56,128]{2,1,0:T(8,128)(2,1)}), bf16[32,56,128]{2,1,0:T(8,128)(2,1)S(1)}, u32[]{:S(2)}, u32[]{:S(2)}) %all-to-all-start.1) | async-done | bytes 458784 | tf_op jit(solution)/shard_map/all_to_all | solution.py:330
  59.1 0.0 copy-done
  59.1 0.0 copy-done.2
  59.1 7.2 %pair_blocks.1 = f32[4,8,8,128]{3,2,1,0:T(8,128)S(1)} custom-call(s32[2]{0:T(128)S(1)} %bitcast.21, s32[1]{0:T(128)} %bitcast.1.place, bf16[32,56,128]{2,1,0:T(8,128)(2,1)S(1)} %all-to-all-done.1.data, bf16[16,48,128]{2,1,0:T(8,128)(2,1)S(1)} %all_to_all.15.slab, f32[32,17,128]{2,1,0:T(8,128)S(1)} %copy.11.screens, bf16[768,256]{1,0:T(8,128)(2,1)S(1)} %copy-done, ...), custom_call_target="tpu_custom_call" | custom-call | tf_op jit(solution)/shard_map/pair_blocks/pallas_call | solution.py:267
  66.4 12.2 %all_to_all.16.parts = f32[32,8,128]{2,1,0:T(8,128)S(1)} all-to-all(f32[32,8,128]{2,1,0:T(8,128)S(1)} %bitcast.17), channel_id=1, replica_groups=mesh['ka'=16,'kp'=32] {'kp'}, dimensions={0} | all-to-all | bytes 262144 | tf_op jit(solution)/shard_map/all_to_all | solution.py:335
  78.6 0.7 last.1
  79.3 3.2 %collective-permute-start = (f32[8,64]{1,0:T(8,128)S(1)}, f32[8,64]{1,0:T(8,128)S(1)}, u32[]{:S(2)}, u32[]{:S(2)}) collective-permute-start(f32[8,64]{1,0:T(8,128)S(1)} %get-tuple-element.5), channel_id=1, source_target_pairs={{12,0},{13,1},{14,32},{15,33},{8,64},{9,65},{10,96},{11,97},{20,12... | collective-permute-start | bytes 6152 | tf_op jit(solution)/shard_map/ppermute | solution.py:348
  82.5 11.6 %collective-permute-done = f32[8,64]{1,0:T(8,128)S(1)} collective-permute-done((f32[8,64]{1,0:T(8,128)S(1)}, f32[8,64]{1,0:T(8,128)S(1)}, u32[]{:S(2)}, u32[]{:S(2)}) %collective-permute-start) | collective-permute-done | bytes 2080 | tf_op jit(solution)/shard_map/ppermute | solution.py:348
  94.1 0.6 copy.13
  (11 shorter events, 0.1 us)
Async XLA Ops:
  0.6 37.1 %copy-start.3 = (bf16[2,16,128]{2,1,0:T(8,128)(2,1)S(1)}, bf16[2,16,128]{2,1,0:T(8,128)(2,1)}, u32[]{:S(2)}) copy-start(bf16[2,16,128]{2,1,0:T(8,128)(2,1)} %param.9) | copy-start | bytes 24580
  38.6 7.2 %copy-start.6 = (s32[512]{0:T(512)S(1)}, s32[512]{0:T(512)}, u32[]{:S(2)}) copy-start(s32[512]{0:T(512)} %param.12) | copy-start | bytes 6148
  38.6 7.3 %copy-start.5 = (f32[32,512]{1,0:T(8,128)S(1)}, f32[32,512]{1,0:T(8,128)}, u32[]{:S(2)}) copy-start(f32[32,512]{1,0:T(8,128)} %param.10) | copy-start | bytes 196612
  38.6 20.5 %all-to-all-start.1 = ((bf16[32,56,128]{2,1,0:T(8,128)(2,1)}), bf16[32,56,128]{2,1,0:T(8,128)(2,1)S(1)}, u32[]{:S(2)}, u32[]{:S(2)}) async-start(bf16[32,56,128]{2,1,0:T(8,128)(2,1)} %second.1), calls=%async_computation.1 | async-start | bytes 917504 | tf_op jit(solution)/shard_map/all_to_all | solution.py:330
  47.2 11.9 %copy-start = (bf16[768,256]{1,0:T(8,128)(2,1)S(1)}, bf16[768,256]{1,0:T(8,128)(2,1)}, u32[]{:S(2)}) copy-start(bf16[768,256]{1,0:T(8,128)(2,1)} %constant.59.clone.matrix) | copy-start | bytes 1179652
  47.2 11.9 %copy-start.1 = (f32[34,8,128]{2,1,0:T(8,128)S(1)}, f32[34,8,128]{2,1,0:T(8,128)}, u32[]{:S(2)}) copy-start(f32[34,8,128]{2,1,0:T(8,128)} %constant.60.clone.table) | copy-start | bytes 417796
  47.2 11.9 %copy-start.2 = (bf16[2,128,128]{2,1,0:T(8,128)(2,1)S(1)}, bf16[2,128,128]{2,1,0:T(8,128)(2,1)}, u32[]{:S(2)}) copy-start(bf16[2,128,128]{2,1,0:T(8,128)(2,1)} %constant.61.clone.order) | copy-start | bytes 196612
  47.2 11.9 %copy-start.4 = (s32[2,1]{0,1:T(1,128)S(1)}, s32[2,1]{0,1:T(1,128)}, u32[]{:S(2)}) copy-start(s32[2,1]{0,1:T(1,128)} %param.11) | copy-start | bytes 28
  79.3 14.8 %collective-permute-start = (f32[8,64]{1,0:T(8,128)S(1)}, f32[8,64]{1,0:T(8,128)S(1)}, u32[]{:S(2)}, u32[]{:S(2)}) collective-permute-start(f32[8,64]{1,0:T(8,128)S(1)} %get-tuple-element.5), channel_id=1, source_target_pairs={{12,0},{13,1},{14,32},{15,33},{8,64},{9,65},{10,96},{11,97},{20,12... | collective-permute-start | bytes 6152 | tf_op jit(solution)/shard_map/ppermute | solution.py:348

commit v5 on v4

--- a/solution.py
+++ b/solution.py
@@ -14,7 +14,7 @@
 INNER = 128
 BLOCK = 56
 SLAB = 48
-GROUPS = OUTER // 2 + 1
+GROUPS = OUTER // 2
 UNROLL = 4
 TURNS = (1, 0, 0, 3)
 BF = jnp.bfloat16
@@ -28,23 +28,37 @@
 
 
 def constants():
+    points = OUTER * INNER
     inner = np.arange(INNER)
-    angle = 2.0 * np.pi * ((inner[:, None] * inner[None, :]) % INNER) / INNER
-    cos, sin = np.cos(angle), np.sin(angle)
-    high, low = split_np(np.block([[cos, -sin], [sin, cos]]))
-    group = np.arange(GROUPS)
-    twist = 2.0 * np.pi * (group[:, None] * inner[None, :]) / (OUTER * INNER)
-    table = np.stack([np.cos(twist), np.sin(twist)], axis=1).reshape(2 * GROUPS, 1, INNER)
-    table = np.broadcast_to(table, (2 * GROUPS, 8, INNER)).astype(np.float32)
+
+    def angle(frequency):
+        return 2.0 * np.pi * ((inner[:, None] * frequency[None, :]) % points) / points
+
+    base = angle(OUTER * inner)
+    group = angle(np.arange(GROUPS))
+    turns = np.concatenate([np.cos(group), np.sin(group), np.zeros((INNER, 96))], axis=1)
+    even = OUTER * np.arange(INNER // 2 + 1)
+    middle = GROUPS + OUTER * np.arange(INNER // 2)
+    zero = np.zeros((INNER, INNER))
+    edge = np.block(
+        [
+            [np.cos(angle(even)), -np.sin(angle(even[1:-1])), zero],
+            [zero, np.cos(angle(middle)), -np.sin(angle(middle))],
+        ]
+    )
+    return (
+        np.stack([np.cos(base), np.sin(base)]).astype(np.float32),
+        turns.astype(np.float32),
+        np.concatenate(split_np(edge), axis=0),
+    )
+
+
+def orders():
     order = np.zeros((2, 128, 128), np.float32)
     for spot in range(64):
         for side in range(2):
             order[side, side * 64 + spot, spot % 8 * 8 + spot // 8] = 1.0
-    return (
-        np.concatenate([high, high, low], axis=0),
-        np.ascontiguousarray(table),
-        order.astype(jnp.bfloat16),
-    )
+    return order.astype(jnp.bfloat16)
 
 
 def real_fft(x):
@@ -107,10 +121,28 @@
         out[i, 40:, :] = index
 
 
-def second_kernel(own, slab, out):
+def turns_kernel(base, turns, edge, out):
+    out[0] = edge[...]
+    for c in range(1, GROUPS):
+        cos = jnp.broadcast_to(turns[:, c : c + 1], (INNER, INNER))
+        sin = jnp.broadcast_to(turns[:, GROUPS + c : GROUPS + c + 1], (INNER, INNER))
+        near = split(base[0] * cos - base[1] * sin)
+        far = base[1] * cos + base[0] * sin
+        back = split(-far)
+        far = split(far)
+        for level in range(2):
+            low, high = level * 256, level * 256 + 128
+            out[c, low:high, :128] = near[level]
+            out[c, low:high, 128:] = back[level]
+            out[c, high : high + 128, :128] = far[level]
+            out[c, high : high + 128, 128:] = near[level]
+
+
+def second_kernel(place, slab, out):
+    own = slab[pl.ds(place[0], 1), :32, :].reshape(32, 128)
     for i in range(out.shape[0]):
         half = i % 2
-        out[i, :32, :] = own[...]
+        out[i, :32, :] = own
         out[i, 32:48, :] = slab[i // 2, half * 16 : half * 16 + 16, :]
         rest = slab[i // 2, 32:48, :].astype(F32)
         index = jnp.broadcast_to(rest[8 + half : 9 + half], (4, 128))
@@ -118,12 +150,9 @@
         out[i, 48:, :] = rest.astype(BF)
 
 
-def last_kernel(parts, applied, adjoint):
-    total = parts[...].sum(axis=0)
-    applied[0] = total[:4, :64]
-    applied[1] = total[:4, 64:]
-    adjoint[:4, :] = total[4:, :64]
-    adjoint[4:, :] = total[4:, 64:]
+def last_kernel(block, out):
+    out[:4, :] = block[:, :64]
+    out[4:, :] = block[:, 64:]
 
 
 def blocks_moved(both):
@@ -143,8 +172,30 @@
 
 
 def block_kernel(
-    pair, place, data, slab, screens, matrix, table, order, out, wide, grid, val, con, acc, weight
+    pair,
+    place,
+    data,
+    slab,
+    screens,
+    turns,
+    order,
+    out,
+    wide,
+    grid,
+    val,
+    con,
+    acc,
+    weight,
+    columns,
+    matrix,
+    sems,
 ):
+    pieces = [
+        pltpu.make_async_copy(turns.at[low:high], matrix.at[low:high], sems.at[i])
+        for i, (low, high) in enumerate(((0, 2), (2, GROUPS)))
+    ]
+    for piece in pieces:
+        piece.start()
     wide[...] = data[:, :48, :].astype(F32)
     for q in range(2):
         weight[q] = screens[pair[q]]
@@ -161,17 +212,11 @@
             for a in range(OUTER)
         ]
         re, im = real_fft(tiles)
-        for c in range(GROUPS):
-            if c == 0:
-                new_re, new_im = re[0], jnp.zeros_like(re[0])
-            elif c == GROUPS - 1:
-                new_re, new_im = re[c] * table[2 * c], -(re[c] * table[2 * c + 1])
-            else:
-                cos, sin = table[2 * c], table[2 * c + 1]
-                new_re = re[c] * cos + im[c] * sin
-                new_im = im[c] * cos - re[c] * sin
-            grid[c, pl.ds(base, 8), :INNER] = new_re
-            grid[c, pl.ds(base, 8), INNER:] = new_im
+        grid[0, pl.ds(base, 8), :INNER] = re[0]
+        grid[0, pl.ds(base, 8), INNER:] = re[GROUPS]
+        for c in range(1, GROUPS):
+            grid[c, pl.ds(base, 8), :INNER] = re[c]
+            grid[c, pl.ds(base, 8), INNER:] = im[c]
 
     def transform_some(i, carry):
         for part in range(UNROLL):
@@ -180,19 +225,21 @@
 
     lax.fori_loop(0, 32 // UNROLL, transform_some, 0)
     acc[...] = jnp.zeros_like(acc)
-
-    def spectra(c, count, slot):
-        x = grid[pl.ds(c, count)].reshape(count * 256, 256)
-        x_high, x_low = split(x)
-        s = dot(jnp.concatenate([x_high, x_low, x_high], axis=1), matrix[...])
-        for part in range(count):
+    inputs = (slab[:, 32:40, :].astype(F32).reshape(128, 128), data[:, 48:52, :].reshape(128, 128))
+    for side in range(2):
+        columns[side] = dot(inputs[side].astype(BF), order[side]).astype(BF)
+
+    def spectra(c, slot):
+        for part in range(2):
+            x_high, x_low = split(grid[c + part])
+            high = matrix[c + part, :256, :]
+            s = dot(x_high, high) + dot(x_low, high) + dot(x_high, matrix[c + part, 256:, :])
             lanes = slice(part * 256, part * 256 + 256)
             for q in range(2):
-                row = part * 256 + q * 128
+                row = q * 128
                 val[slot, q, :, lanes] = jnp.concatenate(split(s[row : row + 64]), axis=0)
                 for side in range(2):
                     w = weight[2 * side + q, pl.ds(c + part, 1), :]
-                    w = jnp.concatenate([w, w], axis=1)
                     rows = slice(side * 128, side * 128 + 128)
                     con[slot, q, rows, lanes] = jnp.concatenate(
                         split(s[row + 64 : row + 128] * w), axis=0
@@ -203,19 +250,20 @@
             acc[q] += dot_t(con[slot, q], val[slot, q])
 
     def four_groups(t, carry):
-        spectra(4 * t + 1, 2, 1)
+        spectra(4 * t + 2, 1)
         contract(0)
-        spectra(4 * t + 3, 2, 0)
+        spectra(4 * t + 4, 0)
         contract(1)
         return carry
 
-    val[0, :, :, 256:] = jnp.zeros((2, 128, 256), BF)
-    con[0, :, :, 256:] = jnp.zeros((2, 256, 256), BF)
-    spectra(0, 1, 0)
-    lax.fori_loop(0, GROUPS // 4, four_groups, 0)
+    pieces[0].wait()
+    spectra(0, 0)
+    pieces[1].wait()
+    lax.fori_loop(0, GROUPS // 4 - 1, four_groups, 0)
+    spectra(GROUPS - 2, 1)
     contract(0)
-
-    inputs = (slab[:, 32:40, :].astype(F32).reshape(128, 128), data[:, 48:52, :].reshape(128, 128))
+    contract(1)
+
     lane = lax.broadcasted_iota(jnp.int32, (64, 128), 1)
     results = []
     for side in range(2):
@@ -225,8 +273,7 @@
             part = part + acc[q, side * 128 + 64 : side * 128 + 128, :]
             twice.append(part + pltpu.roll(part, 64, 1))
         high, low = split(blocks_moved(jnp.where(lane < 64, twice[0], twice[1])))
-        columns = dot(inputs[side].astype(BF), order[side]).astype(BF)
-        results.append(dot_t(columns, high) + dot_t(columns, low))
+        results.append(dot_t(columns[side], high) + dot_t(columns[side], low))
 
     first, full = results
     lane = lax.broadcasted_iota(jnp.int32, (128, 128), 1)
@@ -246,15 +293,20 @@
 
 def make_weight(screen, plane_map, planes, points):
     chosen = screen * (1.0 / (planes * points))
-    group = jnp.arange(GROUPS, dtype=jnp.int32)[:, None]
+    group = jnp.arange(GROUPS + 1, dtype=jnp.int32)[:, None]
     other = points - plane_map
     direct = (plane_map % OUTER)[None, :] == group
-    mirror = ((other % OUTER)[None, :] == group) & (group > 0) & (group < GROUPS - 1)
+    mirror = ((other % OUTER)[None, :] == group) & (other != plane_map)[None, :]
     mask = jnp.concatenate([direct, mirror], axis=1).astype(F32)
     left = mask[None] * jnp.concatenate([chosen, chosen], axis=1)[:, None, :]
     spot = jnp.concatenate([plane_map // OUTER, other // OUTER])
     right = (spot[None, :] == jnp.arange(INNER, dtype=jnp.int32)[:, None]).astype(F32)
-    return jnp.einsum("qcg,hg->qch", left, right, precision=lax.Precision.HIGHEST)
+    full = jnp.einsum("qcg,hg->qch", left, right, precision=lax.Precision.HIGHEST)
+    even, middle = full[:, 0], full[:, GROUPS, : INNER // 2]
+    edge = [even[:, : INNER // 2 + 1], even[:, 1 : INNER // 2], middle, middle]
+    rest = full[:, 1:GROUPS]
+    rest = jnp.concatenate([rest, rest], axis=2)
+    return jnp.concatenate([jnp.concatenate(edge, axis=1)[:, None], rest], axis=1)
 
 
 VMEM = pl.BlockSpec(memory_space=pltpu.VMEM)
@@ -262,12 +314,17 @@
 
 
 def call_kernel(
-    body, name, *inputs, outs, scalars=0, space=VMEM, scratch=(), limit=16, call=pl.pallas_call
+    body, name, *inputs, outs, scalars=0, far=(), scratch=(), limit=16, call=pl.pallas_call
 ):
+    specs = [SMEM] * scalars + [VMEM] * (len(inputs) - scalars)
+    inputs = list(inputs)
+    for i in far:
+        specs[i] = pl.BlockSpec(memory_space=pltpu.HBM)
+        inputs[i] = pltpu.with_memory_space_constraint(inputs[i], pltpu.HBM)
     return call(
         body,
         out_shape=outs,
-        in_specs=[SMEM] * scalars + [space] * (len(inputs) - scalars),
+        in_specs=specs,
         out_specs=jax.tree.map(lambda _: VMEM, outs),
         scratch_shapes=scratch,
         compiler_params=pltpu.CompilerParams(vmem_limit_bytes=limit << 20),
@@ -275,7 +332,17 @@
     )(*inputs)
 
 
-def local_blocks(pair, place, data, slab, screens, call=pl.pallas_call):
+def make_turns(call=pl.pallas_call):
+    return call_kernel(
+        turns_kernel,
+        "turns",
+        *constants(),
+        outs=jax.ShapeDtypeStruct((GROUPS, 512, 256), BF),
+        call=call,
+    )
+
+
+def local_blocks(pair, place, data, slab, screens, turns, call=pl.pallas_call):
     return call_kernel(
         block_kernel,
         "pair_blocks",
@@ -284,7 +351,8 @@
         data,
         slab,
         screens,
-        *constants(),
+        turns,
+        orders(),
         scalars=2,
         outs=jax.ShapeDtypeStruct((4, 8, 8, 128), F32),
         scratch=[
@@ -293,8 +361,12 @@
             pltpu.VMEM((2, 2, 128, 512), BF),
             pltpu.VMEM((2, 2, 256, 512), BF),
             pltpu.VMEM((2, 256, 128), F32),
-            pltpu.VMEM((4, GROUPS, INNER), F32),
+            pltpu.VMEM((4, GROUPS, 2 * INNER), F32),
+            pltpu.VMEM((2, 128, 128), BF),
+            pltpu.VMEM((GROUPS, 512, 256), BF),
+            pltpu.SemaphoreType.DMA((2,)),
         ],
+        far=(5,),
         limit=32,
         call=call,
     )
@@ -303,17 +375,17 @@
 def shards(waves, screen, pair_table, plane_map, trial, probe):
     n_rows = lax.axis_size("ka")
     n_cols = lax.axis_size("kp")
-    own = waves.reshape(32, INNER)
     pair = pair_table.reshape(2)
     place = lax.axis_index("ka").astype(jnp.int32).reshape(1)
 
-    stay = (pair, own, trial.reshape(64, 8).T, probe.transpose(0, 2, 1).reshape(8, 64))
-    stay = [pltpu.with_memory_space_constraint(x, pltpu.HBM) for x in stay]
     out = call_kernel(
         first_kernel,
         "first",
-        *stay,
-        space=pl.BlockSpec(memory_space=pltpu.HBM),
+        pair,
+        waves.reshape(32, INNER),
+        trial.reshape(64, 8).T,
+        probe.transpose(0, 2, 1).reshape(8, 64),
+        far=range(4),
         outs=jax.ShapeDtypeStruct((n_rows, SLAB, 128), BF),
         scratch=[
             pltpu.SMEM((2,), jnp.int32),
@@ -325,28 +397,29 @@
     )
     slab = lax.all_to_all(out, "ka", 0, 0, tiled=True)
     out = call_kernel(
-        second_kernel, "second", own, slab, outs=jax.ShapeDtypeStruct((n_cols, BLOCK, 128), BF)
+        second_kernel,
+        "second",
+        place,
+        slab,
+        scalars=1,
+        outs=jax.ShapeDtypeStruct((n_cols, BLOCK, 128), BF),
     )
     data = lax.all_to_all(out, "kp", 0, 0, tiled=True)
 
     screens = make_weight(screen, plane_map, plane_map.shape[0], OUTER * INNER)
-    out = local_blocks(pair, place, data, slab, screens)
+    out = local_blocks(pair, place, data, slab, screens, make_turns())
 
     parts = lax.all_to_all(out.reshape(n_cols, 8, 128), "kp", 0, 0, tiled=True)
-    applied, adjoint = call_kernel(
-        last_kernel,
-        "last",
-        parts,
-        outs=(jax.ShapeDtypeStruct((2, 4, 64), F32), jax.ShapeDtypeStruct((8, 64), F32)),
-    )
     swap = []
     for a in range(n_rows):
         for b in range(n_rows):
             for c in range(2):
                 spot = (b // 4 + TURNS[a // 4]) % 4 * 8 + (b + 2) % 4 * 2 + c
                 swap.append((a * n_cols + spot, b * n_cols + 2 * a + c))
-    adjoint = lax.ppermute(adjoint, ("ka", "kp"), swap)
-    return applied.transpose(0, 2, 1), adjoint.T.reshape(1, 64, 8)
+    adjoint = lax.ppermute(parts[:, 4:].sum(axis=0), ("ka", "kp"), swap)
+    adjoint = call_kernel(last_kernel, "last", adjoint, outs=jax.ShapeDtypeStruct((8, 64), F32))
+    applied = parts[:, :4].sum(axis=0).reshape(4, 2, 64)
+    return applied.transpose(1, 2, 0), adjoint.T.reshape(1, 64, 8)
 
 
 def solution(mesh):

time: 95 us -> 94.8 us (level)
  blocking collectives: 48.4 us -> 12.2 us
  starting transfers between devices: 10.3 us -> 26 us
  waiting for transfers between devices: 23.3 us -> 38.7 us
  local copies, waits for them, and re-layouts: 0.8 us -> 2.93 us
  other arithmetic: 0.15 us -> 1.67 us
    all_to_all x1 -> x0, blocking collectives: 36.2 us -> none  [shards(): slab = lax.all_to_all(out, 'ka', 0, 0, tiled=True)]
    all_to_all x0 -> x1, waiting for transfers between devices: none -> 19.7 us  [shards(): slab = lax.all_to_all(out, 'ka', 0, 0, tiled=True)]
    all_to_all x0 -> x1, starting transfers between devices: none -> 15.9 us  [shards(): slab = lax.all_to_all(out, 'ka', 0, 0, tiled=True)]
    all_to_all x1, waiting for transfers between devices: 11.7 us -> 8.07 us  [shards(): data = lax.all_to_all(out, 'kp', 0, 0, tiled=True)]
    unnamed x15 -> x16, local copies, waits for them, and re-layouts: 0.63 us -> 2.72 us
    pallas_call x4 -> x5, Pallas kernels: 9.66 us -> 10.6 us  [call_kernel(): call(body, out_shape=outs, in_specs=specs, out_specs=jax.tree.map(lambda...]
  transfers between devices with their start and end apart: 2 -> 3, of which waited for: 2 -> 3; matrix products, arithmetic and copies ran while one was open for 2% -> 4% of each run, Pallas kernels for 0% -> 1%
where the time goes in v5:
time: 94.8 us; the launch traced here: 94.3 us
  waiting for transfers between devices  38.7 us (41%)
  starting transfers between devices  26 us (27%)
  blocking collectives  12.2 us (13%)
  Pallas kernels  10.6 us (11%)
  local copies, waits for them, and re-layouts  2.93 us (3%)
  other arithmetic  1.67 us (2%)
  matrix products  1.25 us (1%)
    all_to_all x1, waiting for transfers between devices, shards(): slab = lax.all_to_all(out, 'ka', 0, 0, tiled=True)  19.7 us
    all_to_all x1, starting transfers between devices, shards(): slab = lax.all_to_all(out, 'ka', 0, 0, tiled=True)  15.9 us
    all_to_all x1, blocking collectives, shards(): parts = lax.all_to_all(out.reshape(n_cols, 8, 128), 'kp', 0, 0, tiled=True)  12.2 us
    ppermute x1, waiting for transfers between devices, shards(): adjoint = lax.ppermute(parts[:, 4:].sum(axis=0), ('ka', 'kp'), swap)  10.9 us
    pallas_call x5, Pallas kernels, call_kernel(): call(body, out_shape=outs, in_specs=specs, out_specs=jax.tree.map(lambda...  10.6 us
    all_to_all x1, waiting for transfers between devices, shards(): data = lax.all_to_all(out, 'kp', 0, 0, tiled=True)  8.07 us
    all_to_all x1, starting transfers between devices, shards(): data = lax.all_to_all(out, 'kp', 0, 0, tiled=True)  6.99 us
    ppermute x1, starting transfers between devices, shards(): adjoint = lax.ppermute(parts[:, 4:].sum(axis=0), ('ka', 'kp'), swap)  3.18 us
  transfers between devices with their start and end apart: 3, of which 3 were waited for; matrix products, arithmetic and copies ran while one was open for 4% of the time, Pallas kernels for 1%

profile of v5, /device:TPU:64, one launch (start us, length us, event | category | flops | bytes accessed | tf_op | source)
XLA Modules:
  0.0 94.3 jit_solution(16479754174677497738)
XLA Ops:
  0.6 1.6 %first.1 = bf16[16,48,128]{2,1,0:T(8,128)(2,1)} custom-call(s32[2]{0:T(128)} %bitcast.23, bf16[32,128]{1,0:T(8,128)(2,1)} %bitcast.27, bf16[8,64]{1,0:T(8,128)(2,1)} %bitcast.29, bf16[8,64]{1,0:T(8,128)(2,1)} %bitcast.30), custom_call_target="tpu_custom_call" | custom-call | tf_op jit(solution)/shard_map/first/pallas_call | solution.py:324
  2.2 15.9 %all-to-all-start = ((bf16[16,48,128]{2,1,0:T(8,128)(2,1)}), bf16[16,48,128]{2,1,0:T(8,128)(2,1)S(1)}, u32[]{:S(2)}, u32[]{:S(2)}) async-start(bf16[16,48,128]{2,1,0:T(8,128)(2,1)} %first.1), calls=%async_computation | async-start | bytes 393216 | tf_op jit(solution)/shard_map/all_to_all | solution.py:398
  18.1 0.0 copy-start.1
  18.1 0.0 copy-start.2
  18.1 0.7 add_select_fusion.1
  18.9 19.7 %all-to-all-done.slab = bf16[16,48,128]{2,1,0:T(8,128)(2,1)S(1)} async-done(((bf16[16,48,128]{2,1,0:T(8,128)(2,1)}), bf16[16,48,128]{2,1,0:T(8,128)(2,1)S(1)}, u32[]{:S(2)}, u32[]{:S(2)}) %all-to-all-start) | async-done | bytes 196640 | tf_op jit(solution)/shard_map/all_to_all | solution.py:398
  38.6 0.8 second.1
  39.5 7.0 %all-to-all-start.1 = ((bf16[32,56,128]{2,1,0:T(8,128)(2,1)}), bf16[32,56,128]{2,1,0:T(8,128)(2,1)S(1)}, u32[]{:S(2)}, u32[]{:S(2)}) async-start(bf16[32,56,128]{2,1,0:T(8,128)(2,1)} %second.1), calls=%async_computation.1 | async-start | bytes 917504 | tf_op jit(solution)/shard_map/all_to_all | solution.py:407
  46.5 0.7 subtract_compare_fusion
  47.3 1.2 %fusion = f32[32,17,128]{2,0,1:T(8,128)S(1)} fusion(f32[32,1024]{1,0:T(8,128)S(1)} %pad_maximum_fusion, f32[17,1024]{1,0:T(8,128)S(1)} %add_convert_fusion, s32[1024]{0:T(1024)S(1)} %pad_add_fusion), kind=kOutput, calls=%fused_computation | convolution fusion | flops 856326144 | bytes 483328 | tf_op jit(solution)/shard_map/qcg,hg->qch/dot_general | solution.py:304
  48.6 0.1 slice.30
  48.6 0.1 pad_maximum_fusion.1
  48.7 0.1 copy.15
  49.0 0.8 turns.2
  49.8 1.9 %copy-done = bf16[16,512,256]{2,1,0:T(8,128)(2,1)} copy-done((bf16[16,512,256]{2,1,0:T(8,128)(2,1)}, bf16[16,512,256]{2,1,0:T(8,128)(2,1)S(1)}, u32[]{:S(2)}) %copy-start) | copy-done | bytes 4194328
  51.7 0.1 maximum_maximum_fusion.screens
  51.8 8.1 %all-to-all-done.1.data = bf16[32,56,128]{2,1,0:T(8,128)(2,1)S(1)} async-done(((bf16[32,56,128]{2,1,0:T(8,128)(2,1)}), bf16[32,56,128]{2,1,0:T(8,128)(2,1)S(1)}, u32[]{:S(2)}, u32[]{:S(2)}) %all-to-all-start.1) | async-done | bytes 458784 | tf_op jit(solution)/shard_map/all_to_all | solution.py:407
  59.9 6.7 %pair_blocks.1 = f32[4,8,8,128]{3,2,1,0:T(8,128)S(1)} custom-call(s32[2]{0:T(128)S(1)} %bitcast.24, s32[1]{0:T(128)} %bitcast.1.place, bf16[32,56,128]{2,1,0:T(8,128)(2,1)S(1)} %all-to-all-done.1.data, bf16[16,48,128]{2,1,0:T(8,128)(2,1)S(1)} %all-to-all-done.slab, f32[32,16,256]{2,1,0:T(8,128)S(1)} %maximum_maximum_fusion.screens, ...), custom_call_target="tpu_custom_call" | custom-call | tf_op jit(solution)/shard_map/pair_blocks/pallas_call | solution.py:324
  66.6 12.2 %all_to_all.15 = f32[32,8,128]{2,1,0:T(8,128)S(1)} all-to-all(f32[32,8,128]{2,1,0:T(8,128)S(1)} %bitcast.22), channel_id=1, replica_groups=mesh['ka'=16,'kp'=32] {'kp'}, dimensions={0} | all-to-all | bytes 262144 | tf_op jit(solution)/shard_map/all_to_all | solution.py:412
  78.9 3.2 %collective-permute-start = (f32[4,128]{1,0:T(4,128)S(1)}, f32[4,128]{1,0:T(4,128)S(1)}, u32[]{:S(2)}, u32[]{:S(2)}) collective-permute-start(f32[4,128]{1,0:T(4,128)S(1)} %get-tuple-element.4), channel_id=1, source_target_pairs={{12,0},{13,1},{14,32},{15,33},{8,64},{9,65},{10,96},{11,97},{20,12... | collective-permute-start | bytes 6152 | tf_op jit(solution)/shard_map/ppermute | solution.py:419
  82.1 0.1 reshape.76
  82.1 0.6 copy.14
  82.7 10.9 %collective-permute-done.block = f32[4,128]{1,0:T(4,128)S(1)} collective-permute-done((f32[4,128]{1,0:T(4,128)S(1)}, f32[4,128]{1,0:T(4,128)S(1)}, u32[]{:S(2)}, u32[]{:S(2)}) %collective-permute-start) | collective-permute-done | bytes 2080 | tf_op jit(solution)/shard_map/ppermute | solution.py:419
  93.7 0.7 last.1
  (21 shorter events, 0.2 us)
Async XLA Ops:
  0.6 46.6 %copy-start.6 = (f32[32,512]{1,0:T(8,128)S(1)}, f32[32,512]{1,0:T(8,128)}, u32[]{:S(2)}) copy-start(f32[32,512]{1,0:T(8,128)} %param.11) | copy-start | bytes 196612
  2.2 36.4 %all-to-all-start = ((bf16[16,48,128]{2,1,0:T(8,128)(2,1)}), bf16[16,48,128]{2,1,0:T(8,128)(2,1)S(1)}, u32[]{:S(2)}, u32[]{:S(2)}) async-start(bf16[16,48,128]{2,1,0:T(8,128)(2,1)} %first.1), calls=%async_computation | async-start | bytes 393216 | tf_op jit(solution)/shard_map/all_to_all | solution.py:398
  18.1 30.8 %copy-start.1 = (bf16[512,256]{1,0:T(8,128)(2,1)S(1)}, bf16[512,256]{1,0:T(8,128)(2,1)}, u32[]{:S(2)}) copy-start(bf16[512,256]{1,0:T(8,128)(2,1)} %constant.62.clone.edge) | copy-start | bytes 786436
  18.1 30.8 %copy-start.2 = (f32[2,128,128]{2,1,0:T(8,128)S(1)}, f32[2,128,128]{2,1,0:T(8,128)}, u32[]{:S(2)}) copy-start(f32[2,128,128]{2,1,0:T(8,128)} %constant.60.clone.base) | copy-start | bytes 393220
  18.1 30.8 %copy-start.4 = (f32[128,128]{1,0:T(8,128)S(1)}, f32[128,128]{1,0:T(8,128)}, u32[]{:S(2)}) copy-start(f32[128,128]{1,0:T(8,128)} %constant.61.clone.turns) | copy-start | bytes 196612
  39.5 20.4 %all-to-all-start.1 = ((bf16[32,56,128]{2,1,0:T(8,128)(2,1)}), bf16[32,56,128]{2,1,0:T(8,128)(2,1)S(1)}, u32[]{:S(2)}, u32[]{:S(2)}) async-start(bf16[32,56,128]{2,1,0:T(8,128)(2,1)} %second.1), calls=%async_computation.1 | async-start | bytes 917504 | tf_op jit(solution)/shard_map/all_to_all | solution.py:407
  48.9 10.9 %copy-start.3 = (bf16[2,128,128]{2,1,0:T(8,128)(2,1)S(1)}, bf16[2,128,128]{2,1,0:T(8,128)(2,1)}, u32[]{:S(2)}) copy-start(bf16[2,128,128]{2,1,0:T(8,128)(2,1)} %constant.63.clone.order) | copy-start | bytes 196612
  48.9 10.9 %copy-start.5 = (s32[2,1]{0,1:T(1,128)S(1)}, s32[2,1]{0,1:T(1,128)}, u32[]{:S(2)}) copy-start(s32[2,1]{0,1:T(1,128)} %param.12) | copy-start | bytes 28
  49.8 1.9 %copy-start = (bf16[16,512,256]{2,1,0:T(8,128)(2,1)}, bf16[16,512,256]{2,1,0:T(8,128)(2,1)S(1)}, u32[]{:S(2)}) copy-start(bf16[16,512,256]{2,1,0:T(8,128)(2,1)S(1)} %turns.2) | copy-start | bytes 12582916
  78.9 14.8 %collective-permute-start = (f32[4,128]{1,0:T(4,128)S(1)}, f32[4,128]{1,0:T(4,128)S(1)}, u32[]{:S(2)}, u32[]{:S(2)}) collective-permute-start(f32[4,128]{1,0:T(4,128)S(1)} %get-tuple-element.4), channel_id=1, source_target_pairs={{12,0},{13,1},{14,32},{15,33},{8,64},{9,65},{10,96},{11,97},{20,12... | collective-permute-start | bytes 6152 | tf_op jit(solution)/shard_map/ppermute | solution.py:419

commit v6 on v5

--- a/solution.py
+++ b/solution.py
@@ -12,8 +12,8 @@
 NC = 8
 OUTER = 32
 INNER = 128
-BLOCK = 56
-SLAB = 48
+BLOCK = 13
+SLAB = 11
 GROUPS = OUTER // 2
 UNROLL = 4
 TURNS = (1, 0, 0, 3)
@@ -113,12 +113,11 @@
     for copy in copies:
         copy.wait()
     side = jnp.concatenate([trial_here[...], probe_here[...]], axis=1)
-    spot = lax.broadcasted_iota(jnp.int32, (8, 128), 0)
+    spot = lax.broadcasted_iota(jnp.int32, (4, 128), 0)
     index = jnp.where(spot == 0, pair_here[0], pair_here[1]).astype(F32).astype(BF)
+    rows = [own_here[4 * i : 4 * i + 4, :] for i in range(8)] + [side[:4], side[4:], index]
     for i in range(out.shape[0]):
-        out[i, :32, :] = own_here[...]
-        out[i, 32:40, :] = side
-        out[i, 40:, :] = index
+        out[i, :, :] = rows[i % SLAB]
 
 
 def turns_kernel(base, turns, edge, out):
@@ -139,15 +138,16 @@
 
 
 def second_kernel(place, slab, out):
-    own = slab[pl.ds(place[0], 1), :32, :].reshape(32, 128)
-    for i in range(out.shape[0]):
-        half = i % 2
-        out[i, :32, :] = own
-        out[i, 32:48, :] = slab[i // 2, half * 16 : half * 16 + 16, :]
-        rest = slab[i // 2, 32:48, :].astype(F32)
-        index = jnp.broadcast_to(rest[8 + half : 9 + half], (4, 128))
-        rest = jnp.concatenate([rest[half * 4 : half * 4 + 4], index], axis=0)
-        out[i, 48:, :] = rest.astype(BF)
+    own = slab[pl.ds(place[0] * SLAB, 8)]
+    lane = lax.broadcasted_iota(jnp.int32, (4, 128), 1)
+    for i in range(out.shape[0] // BLOCK):
+        half, start = i % 2, i // 2 * SLAB
+        index = slab[start + 10].astype(F32)[half : half + 1]
+        index = jnp.broadcast_to(index, (4, 128))
+        last = jnp.where(lane < 64, index, slab[start + 8 + half].astype(F32))
+        out[i * BLOCK : i * BLOCK + 8] = own
+        out[i * BLOCK + 8 : i * BLOCK + 12] = slab[start + half * 4 : start + half * 4 + 4]
+        out[i * BLOCK + 12] = last.astype(BF)
 
 
 def last_kernel(block, out):
@@ -190,16 +190,18 @@
     matrix,
     sems,
 ):
-    pieces = [
-        pltpu.make_async_copy(turns.at[low:high], matrix.at[low:high], sems.at[i])
-        for i, (low, high) in enumerate(((0, 2), (2, GROUPS)))
-    ]
-    for piece in pieces:
-        piece.start()
-    wide[...] = data[:, :48, :].astype(F32)
+    def piece(i):
+        part = pl.ds(2 * i, 2)
+        return pltpu.make_async_copy(turns.at[part], matrix.at[part], sems.at[i])
+
+    for i in range(GROUPS // 2):
+        piece(i).start()
+    parts = data[...].reshape(OUTER, BLOCK, 4, 128)
+    for i in range(12):
+        wide[:, 4 * i : 4 * i + 4, :] = parts[:, i].astype(F32)
     for q in range(2):
         weight[q] = screens[pair[q]]
-        other = data[pl.ds(2 * place[0] + q, 1), 52:56, :].astype(F32)
+        other = data[(2 * place[0] + q) * BLOCK + 12].astype(F32)[:, :64]
         weight[2 + q] = screens[jnp.max(other).astype(jnp.int32)]
 
     def transform(i):
@@ -225,7 +227,8 @@
 
     lax.fori_loop(0, 32 // UNROLL, transform_some, 0)
     acc[...] = jnp.zeros_like(acc)
-    inputs = (slab[:, 32:40, :].astype(F32).reshape(128, 128), data[:, 48:52, :].reshape(128, 128))
+    side = slab[...].reshape(16, SLAB, 4, 128)[:, 8:10].reshape(128, 128)
+    inputs = (side, parts[:, 12].reshape(128, 128))
     for side in range(2):
         columns[side] = dot(inputs[side].astype(BF), order[side]).astype(BF)
 
@@ -250,16 +253,18 @@
             acc[q] += dot_t(con[slot, q], val[slot, q])
 
     def four_groups(t, carry):
+        piece(2 * t + 1).wait()
+        piece(2 * t + 2).wait()
         spectra(4 * t + 2, 1)
         contract(0)
         spectra(4 * t + 4, 0)
         contract(1)
         return carry
 
-    pieces[0].wait()
+    piece(0).wait()
     spectra(0, 0)
-    pieces[1].wait()
     lax.fori_loop(0, GROUPS // 4 - 1, four_groups, 0)
+    piece(GROUPS // 2 - 1).wait()
     spectra(GROUPS - 2, 1)
     contract(0)
     contract(1)
@@ -364,7 +369,7 @@
             pltpu.VMEM((4, GROUPS, 2 * INNER), F32),
             pltpu.VMEM((2, 128, 128), BF),
             pltpu.VMEM((GROUPS, 512, 256), BF),
-            pltpu.SemaphoreType.DMA((2,)),
+            pltpu.SemaphoreType.DMA((GROUPS // 2,)),
         ],
         far=(5,),
         limit=32,
@@ -386,7 +391,7 @@
         trial.reshape(64, 8).T,
         probe.transpose(0, 2, 1).reshape(8, 64),
         far=range(4),
-        outs=jax.ShapeDtypeStruct((n_rows, SLAB, 128), BF),
+        outs=jax.ShapeDtypeStruct((n_rows * SLAB, 4, 128), BF),
         scratch=[
             pltpu.SMEM((2,), jnp.int32),
             pltpu.VMEM((32, 128), BF),
@@ -402,7 +407,7 @@
         place,
         slab,
         scalars=1,
-        outs=jax.ShapeDtypeStruct((n_cols, BLOCK, 128), BF),
+        outs=jax.ShapeDtypeStruct((n_cols * BLOCK, 4, 128), BF),
     )
     data = lax.all_to_all(out, "kp", 0, 0, tiled=True)
 

time: 94.8 us -> 93.5 us (0.986)
  waiting for transfers between devices: 38.7 us -> 37.4 us
    all_to_all x1, waiting for transfers between devices: 19.7 us -> 18.4 us  [shards(): slab = lax.all_to_all(out, 'ka', 0, 0, tiled=True)]
where the time goes in v6:
time: 93.5 us; the launch traced here: 93.1 us
  waiting for transfers between devices  37.4 us (40%)
  starting transfers between devices  26 us (28%)
  blocking collectives  12.2 us (13%)
  Pallas kernels  10.8 us (12%)
  local copies, waits for them, and re-layouts  2.93 us (3%)
  other arithmetic  1.67 us (2%)
  matrix products  1.25 us (1%)
    all_to_all x1, waiting for transfers between devices, shards(): slab = lax.all_to_all(out, 'ka', 0, 0, tiled=True)  18.4 us
    all_to_all x1, starting transfers between devices, shards(): slab = lax.all_to_all(out, 'ka', 0, 0, tiled=True)  15.9 us
    all_to_all x1, blocking collectives, shards(): parts = lax.all_to_all(out.reshape(n_cols, 8, 128), 'kp', 0, 0, tiled=True)  12.2 us
    ppermute x1, waiting for transfers between devices, shards(): adjoint = lax.ppermute(parts[:, 4:].sum(axis=0), ('ka', 'kp'), swap)  11 us
    pallas_call x5, Pallas kernels, call_kernel(): call(body, out_shape=outs, in_specs=specs, out_specs=jax.tree.map(lambda...  10.8 us
    all_to_all x1, waiting for transfers between devices, shards(): data = lax.all_to_all(out, 'kp', 0, 0, tiled=True)  8.08 us
    all_to_all x1, starting transfers between devices, shards(): data = lax.all_to_all(out, 'kp', 0, 0, tiled=True)  6.99 us
    ppermute x1, starting transfers between devices, shards(): adjoint = lax.ppermute(parts[:, 4:].sum(axis=0), ('ka', 'kp'), swap)  3.14 us
  transfers between devices with their start and end apart: 3, of which 3 were waited for; matrix products, arithmetic and copies ran while one was open for 4% of the time, Pallas kernels for 1%

profile of v6, /device:TPU:64, one launch (start us, length us, event | category | flops | bytes accessed | tf_op | source)
XLA Modules:
  0.0 93.1 jit_solution(14490174493260860251)
XLA Ops:
  0.6 1.6 %first.1 = bf16[176,4,128]{2,1,0:T(4,128)(2,1)} custom-call(s32[2]{0:T(128)} %bitcast.23, bf16[32,128]{1,0:T(8,128)(2,1)} %bitcast.27, bf16[8,64]{1,0:T(8,128)(2,1)} %bitcast.29, bf16[8,64]{1,0:T(8,128)(2,1)} %bitcast.30), custom_call_target="tpu_custom_call" | custom-call | tf_op jit(solution)/shard_map/first/pallas_call | solution.py:329
  2.2 15.9 %all-to-all-start = ((bf16[176,4,128]{2,1,0:T(4,128)(2,1)}), bf16[176,4,128]{2,1,0:T(4,128)(2,1)S(1)}, u32[]{:S(2)}, u32[]{:S(2)}) async-start(bf16[176,4,128]{2,1,0:T(4,128)(2,1)} %first.1), calls=%async_computation | async-start | bytes 360448 | tf_op jit(solution)/shard_map/all_to_all | solution.py:403
  18.1 0.0 copy-start.1
  18.1 0.0 copy-start.2
  18.1 0.7 subtract_compare_fusion
  18.9 0.7 add_select_fusion.1
  19.6 18.4 %all-to-all-done.slab = bf16[176,4,128]{2,1,0:T(4,128)(2,1)S(1)} async-done(((bf16[176,4,128]{2,1,0:T(4,128)(2,1)}), bf16[176,4,128]{2,1,0:T(4,128)(2,1)S(1)}, u32[]{:S(2)}, u32[]{:S(2)}) %all-to-all-start) | async-done | bytes 180256 | tf_op jit(solution)/shard_map/all_to_all | solution.py:403
  38.0 0.9 second.1
  38.8 7.0 %all-to-all-start.1 = ((bf16[416,4,128]{2,1,0:T(4,128)(2,1)}), bf16[416,4,128]{2,1,0:T(4,128)(2,1)S(1)}, u32[]{:S(2)}, u32[]{:S(2)}) async-start(bf16[416,4,128]{2,1,0:T(4,128)(2,1)} %second.1), calls=%async_computation.1 | async-start | bytes 851968 | tf_op jit(solution)/shard_map/all_to_all | solution.py:412
  45.9 1.2 %fusion = f32[32,17,128]{2,0,1:T(8,128)S(1)} fusion(f32[32,1024]{1,0:T(8,128)S(1)} %pad_maximum_fusion, f32[17,1024]{1,0:T(8,128)S(1)} %add_convert_fusion, s32[1024]{0:T(1024)S(1)} %pad_add_fusion), kind=kOutput, calls=%fused_computation | convolution fusion | flops 856326144 | bytes 483328 | tf_op jit(solution)/shard_map/qcg,hg->qch/dot_general | solution.py:309
  47.2 0.1 slice.30
  47.3 0.1 pad_maximum_fusion.1
  47.4 0.1 copy.15
  47.6 0.8 turns.2
  48.5 1.9 %copy-done = bf16[16,512,256]{2,1,0:T(8,128)(2,1)} copy-done((bf16[16,512,256]{2,1,0:T(8,128)(2,1)}, bf16[16,512,256]{2,1,0:T(8,128)(2,1)S(1)}, u32[]{:S(2)}) %copy-start) | copy-done | bytes 4194328
  50.4 0.1 maximum_maximum_fusion.screens
  50.5 8.1 %all-to-all-done.1.data = bf16[416,4,128]{2,1,0:T(4,128)(2,1)S(1)} async-done(((bf16[416,4,128]{2,1,0:T(4,128)(2,1)}), bf16[416,4,128]{2,1,0:T(4,128)(2,1)S(1)}, u32[]{:S(2)}, u32[]{:S(2)}) %all-to-all-start.1) | async-done | bytes 426016 | tf_op jit(solution)/shard_map/all_to_all | solution.py:412
  58.6 6.8 %pair_blocks.1 = f32[4,8,8,128]{3,2,1,0:T(8,128)S(1)} custom-call(s32[2]{0:T(128)S(1)} %bitcast.24, s32[1]{0:T(128)} %bitcast.1.place, bf16[416,4,128]{2,1,0:T(4,128)(2,1)S(1)} %all-to-all-done.1.data, bf16[176,4,128]{2,1,0:T(4,128)(2,1)S(1)} %all-to-all-done.slab, f32[32,16,256]{2,1,0:T(8,128)S(1)} %maximum_maximum_fusion.screens, ...), custom_call_target="tpu_custom_call" | custom-call | tf_op jit(solution)/shard_map/pair_blocks/pallas_call | solution.py:329
  65.4 12.2 %all_to_all.15 = f32[32,8,128]{2,1,0:T(8,128)S(1)} all-to-all(f32[32,8,128]{2,1,0:T(8,128)S(1)} %bitcast.22), channel_id=1, replica_groups=mesh['ka'=16,'kp'=32] {'kp'}, dimensions={0} | all-to-all | bytes 262144 | tf_op jit(solution)/shard_map/all_to_all | solution.py:417
  77.6 3.1 %collective-permute-start = (f32[4,128]{1,0:T(4,128)S(1)}, f32[4,128]{1,0:T(4,128)S(1)}, u32[]{:S(2)}, u32[]{:S(2)}) collective-permute-start(f32[4,128]{1,0:T(4,128)S(1)} %get-tuple-element.4), channel_id=1, source_target_pairs={{12,0},{13,1},{14,32},{15,33},{8,64},{9,65},{10,96},{11,97},{20,12... | collective-permute-start | bytes 6152 | tf_op jit(solution)/shard_map/ppermute | solution.py:424
  80.8 0.1 reshape.76
  80.9 0.6 copy.14
  81.5 11.0 %collective-permute-done.block = f32[4,128]{1,0:T(4,128)S(1)} collective-permute-done((f32[4,128]{1,0:T(4,128)S(1)}, f32[4,128]{1,0:T(4,128)S(1)}, u32[]{:S(2)}, u32[]{:S(2)}) %collective-permute-start) | collective-permute-done | bytes 2080 | tf_op jit(solution)/shard_map/ppermute | solution.py:424
  92.4 0.7 last.1
  (21 shorter events, 0.2 us)
Async XLA Ops:
  0.6 45.3 %copy-start.6 = (f32[32,512]{1,0:T(8,128)S(1)}, f32[32,512]{1,0:T(8,128)}, u32[]{:S(2)}) copy-start(f32[32,512]{1,0:T(8,128)} %param.11) | copy-start | bytes 196612
  2.2 35.8 %all-to-all-start = ((bf16[176,4,128]{2,1,0:T(4,128)(2,1)}), bf16[176,4,128]{2,1,0:T(4,128)(2,1)S(1)}, u32[]{:S(2)}, u32[]{:S(2)}) async-start(bf16[176,4,128]{2,1,0:T(4,128)(2,1)} %first.1), calls=%async_computation | async-start | bytes 360448 | tf_op jit(solution)/shard_map/all_to_all | solution.py:403
  18.1 29.5 %copy-start.1 = (bf16[512,256]{1,0:T(8,128)(2,1)S(1)}, bf16[512,256]{1,0:T(8,128)(2,1)}, u32[]{:S(2)}) copy-start(bf16[512,256]{1,0:T(8,128)(2,1)} %constant.62.clone.edge) | copy-start | bytes 786436
  18.1 29.5 %copy-start.2 = (f32[2,128,128]{2,1,0:T(8,128)S(1)}, f32[2,128,128]{2,1,0:T(8,128)}, u32[]{:S(2)}) copy-start(f32[2,128,128]{2,1,0:T(8,128)} %constant.60.clone.base) | copy-start | bytes 393220
  18.1 29.5 %copy-start.4 = (f32[128,128]{1,0:T(8,128)S(1)}, f32[128,128]{1,0:T(8,128)}, u32[]{:S(2)}) copy-start(f32[128,128]{1,0:T(8,128)} %constant.61.clone.turns) | copy-start | bytes 196612
  38.8 19.7 %all-to-all-start.1 = ((bf16[416,4,128]{2,1,0:T(4,128)(2,1)}), bf16[416,4,128]{2,1,0:T(4,128)(2,1)S(1)}, u32[]{:S(2)}, u32[]{:S(2)}) async-start(bf16[416,4,128]{2,1,0:T(4,128)(2,1)} %second.1), calls=%async_computation.1 | async-start | bytes 851968 | tf_op jit(solution)/shard_map/all_to_all | solution.py:412
  47.6 10.9 %copy-start.3 = (bf16[2,128,128]{2,1,0:T(8,128)(2,1)S(1)}, bf16[2,128,128]{2,1,0:T(8,128)(2,1)}, u32[]{:S(2)}) copy-start(bf16[2,128,128]{2,1,0:T(8,128)(2,1)} %constant.63.clone.order) | copy-start | bytes 196612
  47.6 10.9 %copy-start.5 = (s32[2,1]{0,1:T(1,128)S(1)}, s32[2,1]{0,1:T(1,128)}, u32[]{:S(2)}) copy-start(s32[2,1]{0,1:T(1,128)} %param.12) | copy-start | bytes 28
  48.5 1.9 %copy-start = (bf16[16,512,256]{2,1,0:T(8,128)(2,1)}, bf16[16,512,256]{2,1,0:T(8,128)(2,1)S(1)}, u32[]{:S(2)}) copy-start(bf16[16,512,256]{2,1,0:T(8,128)(2,1)S(1)} %turns.2) | copy-start | bytes 12582916
  77.6 14.8 %collective-permute-start = (f32[4,128]{1,0:T(4,128)S(1)}, f32[4,128]{1,0:T(4,128)S(1)}, u32[]{:S(2)}, u32[]{:S(2)}) collective-permute-start(f32[4,128]{1,0:T(4,128)S(1)} %get-tuple-element.4), channel_id=1, source_target_pairs={{12,0},{13,1},{14,32},{15,33},{8,64},{9,65},{10,96},{11,97},{20,12... | collective-permute-start | bytes 6152 | tf_op jit(solution)/shard_map/ppermute | solution.py:424

commit v7 on v6

--- a/solution.py
+++ b/solution.py
@@ -137,8 +137,8 @@
             out[c, high : high + 128, 128:] = near[level]
 
 
-def second_kernel(place, slab, out):
-    own = slab[pl.ds(place[0] * SLAB, 8)]
+def second_kernel(slab, out):
+    own = slab[pl.ds(lax.axis_index("ka") * SLAB, 8)]
     lane = lax.broadcasted_iota(jnp.int32, (4, 128), 1)
     for i in range(out.shape[0] // BLOCK):
         half, start = i % 2, i // 2 * SLAB
@@ -173,7 +173,6 @@
 
 def block_kernel(
     pair,
-    place,
     data,
     slab,
     screens,
@@ -201,7 +200,7 @@
         wide[:, 4 * i : 4 * i + 4, :] = parts[:, i].astype(F32)
     for q in range(2):
         weight[q] = screens[pair[q]]
-        other = data[(2 * place[0] + q) * BLOCK + 12].astype(F32)[:, :64]
+        other = data[(2 * lax.axis_index("ka") + q) * BLOCK + 12].astype(F32)[:, :64]
         weight[2 + q] = screens[jnp.max(other).astype(jnp.int32)]
 
     def transform(i):
@@ -288,7 +287,7 @@
     first = first.reshape(16, 8, 128)
     for i in range(32):
         out[i // 8, i % 8, :4, :] = first[i // 2, i % 2 * 4 : i % 2 * 4 + 4, :]
-    zone = place[0] // 4
+    zone = lax.axis_index("ka") // 4
     turn = jnp.where(zone == 0, TURNS[0], jnp.where(zone == 3, TURNS[3], 0))
     for i in range(32):
         spot = jnp.bitwise_and(i // 8 + turn, 3)
@@ -337,28 +336,27 @@
     )(*inputs)
 
 
-def make_turns(call=pl.pallas_call):
+def make_turns(tables, call=pl.pallas_call):
     return call_kernel(
         turns_kernel,
         "turns",
-        *constants(),
+        *tables,
         outs=jax.ShapeDtypeStruct((GROUPS, 512, 256), BF),
         call=call,
     )
 
 
-def local_blocks(pair, place, data, slab, screens, turns, call=pl.pallas_call):
+def local_blocks(pair, data, slab, screens, turns, call=pl.pallas_call):
     return call_kernel(
         block_kernel,
         "pair_blocks",
         pair,
-        place,
         data,
         slab,
         screens,
         turns,
         orders(),
-        scalars=2,
+        scalars=1,
         outs=jax.ShapeDtypeStruct((4, 8, 8, 128), F32),
         scratch=[
             pltpu.VMEM((OUTER, 48, INNER), F32),
@@ -371,7 +369,7 @@
             pltpu.VMEM((GROUPS, 512, 256), BF),
             pltpu.SemaphoreType.DMA((GROUPS // 2,)),
         ],
-        far=(5,),
+        far=(4,),
         limit=32,
         call=call,
     )
@@ -381,7 +379,6 @@
     n_rows = lax.axis_size("ka")
     n_cols = lax.axis_size("kp")
     pair = pair_table.reshape(2)
-    place = lax.axis_index("ka").astype(jnp.int32).reshape(1)
 
     out = call_kernel(
         first_kernel,
@@ -401,18 +398,18 @@
         ],
     )
     slab = lax.all_to_all(out, "ka", 0, 0, tiled=True)
+    tables = [jnp.asarray(table) for table in constants()]
+    slab, plane_map, screen, tables = lax.optimization_barrier((slab, plane_map, screen, tables))
     out = call_kernel(
         second_kernel,
         "second",
-        place,
         slab,
-        scalars=1,
         outs=jax.ShapeDtypeStruct((n_cols * BLOCK, 4, 128), BF),
     )
     data = lax.all_to_all(out, "kp", 0, 0, tiled=True)
 
     screens = make_weight(screen, plane_map, plane_map.shape[0], OUTER * INNER)
-    out = local_blocks(pair, place, data, slab, screens, make_turns())
+    out = local_blocks(pair, data, slab, screens, make_turns(tables))
 
     parts = lax.all_to_all(out.reshape(n_cols, 8, 128), "kp", 0, 0, tiled=True)
     swap = []

time: 93.5 us -> 94 us (level)
  blocking collectives: 12.2 us -> 47.7 us
  waiting for transfers between devices: 37.4 us -> 19 us
  starting transfers between devices: 26 us -> 10.1 us
    all_to_all x0 -> x1, blocking collectives: none -> 35.5 us  [shards(): slab = lax.all_to_all(out, 'ka', 0, 0, tiled=True)]
    all_to_all x1 -> x0, waiting for transfers between devices: 18.4 us -> none  [shards(): slab = lax.all_to_all(out, 'ka', 0, 0, tiled=True)]
    all_to_all x1 -> x0, starting transfers between devices: 15.9 us -> none  [shards(): slab = lax.all_to_all(out, 'ka', 0, 0, tiled=True)]
  transfers between devices with their start and end apart: 3 -> 2, of which waited for: 3 -> 2; matrix products, arithmetic and copies ran while one was open for 4% -> 3% of each run, Pallas kernels for 1% -> 1%
where the time goes in v7:
time: 94 us; the launch traced here: 93.6 us
  blocking collectives  47.7 us (51%)
  waiting for transfers between devices  19 us (20%)
  Pallas kernels  10.1 us (11%)
  starting transfers between devices  10.1 us (11%)
  local copies, waits for them, and re-layouts  2.91 us (3%)
  other arithmetic  1.67 us (2%)
  matrix products  1.24 us (1%)
    all_to_all x1, blocking collectives, shards(): slab = lax.all_to_all(out, 'ka', 0, 0, tiled=True)  35.5 us
    all_to_all x1, blocking collectives, shards(): parts = lax.all_to_all(out.reshape(n_cols, 8, 128), 'kp', 0, 0, tiled=True)  12.2 us
    ppermute x1, waiting for transfers between devices, shards(): adjoint = lax.ppermute(parts[:, 4:].sum(axis=0), ('ka', 'kp'), swap)  11 us
    pallas_call x5, Pallas kernels, call_kernel(): call(body, out_shape=outs, in_specs=specs, out_specs=jax.tree.map(lambda...  10.1 us
    all_to_all x1, waiting for transfers between devices, shards(): data = lax.all_to_all(out, 'kp', 0, 0, tiled=True)  8.08 us
    all_to_all x1, starting transfers between devices, shards(): data = lax.all_to_all(out, 'kp', 0, 0, tiled=True)  6.99 us
    ppermute x1, starting transfers between devices, shards(): adjoint = lax.ppermute(parts[:, 4:].sum(axis=0), ('ka', 'kp'), swap)  3.14 us
    unnamed x16, local copies, waits for them, and re-layouts  2.71 us
  transfers between devices with their start and end apart: 2, of which 2 were waited for; matrix products, arithmetic and copies ran while one was open for 3% of the time, Pallas kernels for 1%

profile of v7, /device:TPU:64, one launch (start us, length us, event | category | flops | bytes accessed | tf_op | source)
XLA Modules:
  0.0 93.6 jit_solution(11285387204057507612)
XLA Ops:
  0.6 0.0 copy-start.6
  0.6 0.9 first.1
  1.6 35.5 %all_to_all.15.slab = bf16[176,4,128]{2,1,0:T(4,128)(2,1)S(1)} all-to-all(bf16[176,4,128]{2,1,0:T(4,128)(2,1)S(1)} %first.1), channel_id=1, replica_groups=mesh['ka'=16,'kp'=32] {'ka'}, dimensions={0} | all-to-all | bytes 360448 | tf_op jit(solution)/shard_map/all_to_all | solution.py:400
  37.1 0.7 subtract_compare_fusion
  37.8 0.7 add_select_fusion.1
  38.5 0.9 second.1
  39.4 7.0 %all-to-all-start.1 = ((bf16[416,4,128]{2,1,0:T(4,128)(2,1)}), bf16[416,4,128]{2,1,0:T(4,128)(2,1)S(1)}, u32[]{:S(2)}, u32[]{:S(2)}) async-start(bf16[416,4,128]{2,1,0:T(4,128)(2,1)} %second.1), calls=%async_computation.1 | async-start | bytes 851968 | tf_op jit(solution)/shard_map/all_to_all | solution.py:409
  46.5 1.2 %fusion = f32[32,17,128]{2,0,1:T(8,128)S(1)} fusion(f32[32,1024]{1,0:T(8,128)S(1)} %pad_maximum_fusion, f32[17,1024]{1,0:T(8,128)S(1)} %add_convert_fusion, s32[1024]{0:T(1024)S(1)} %pad_add_fusion), kind=kOutput, calls=%fused_computation | convolution fusion | flops 856326144 | bytes 483328 | tf_op jit(solution)/shard_map/qcg,hg->qch/dot_general | solution.py:308
  47.8 0.1 slice.30
  47.9 0.1 pad_maximum_fusion.1
  48.0 0.1 copy.15
  48.2 0.0 copy-start.3
  48.2 0.0 copy-start.5
  48.2 0.8 turns.1
  49.0 1.9 %copy-done = bf16[16,512,256]{2,1,0:T(8,128)(2,1)} copy-done((bf16[16,512,256]{2,1,0:T(8,128)(2,1)}, bf16[16,512,256]{2,1,0:T(8,128)(2,1)S(1)}, u32[]{:S(2)}) %copy-start) | copy-done | bytes 4194328
  51.0 0.1 maximum_maximum_fusion.screens
  51.0 8.1 %all-to-all-done.1.data = bf16[416,4,128]{2,1,0:T(4,128)(2,1)S(1)} async-done(((bf16[416,4,128]{2,1,0:T(4,128)(2,1)}), bf16[416,4,128]{2,1,0:T(4,128)(2,1)S(1)}, u32[]{:S(2)}, u32[]{:S(2)}) %all-to-all-start.1) | async-done | bytes 426016 | tf_op jit(solution)/shard_map/all_to_all | solution.py:409
  59.1 6.8 %pair_blocks.1 = f32[4,8,8,128]{3,2,1,0:T(8,128)S(1)} custom-call(s32[2]{0:T(128)S(1)} %bitcast.23, bf16[416,4,128]{2,1,0:T(4,128)(2,1)S(1)} %all-to-all-done.1.data, bf16[176,4,128]{2,1,0:T(4,128)(2,1)S(1)} %all_to_all.15.slab, f32[32,16,256]{2,1,0:T(8,128)S(1)} %maximum_maximum_fusion.screens, bf16[16,512,256]{2,1,0:T(8,128)(2,1)} %copy-done, ...), custom_call_target="tpu_custom_call" | custom-call | tf_op jit(solution)/shard_map/pair_blocks/pallas_call | solution.py:328
  66.0 12.2 %all_to_all.16 = f32[32,8,128]{2,1,0:T(8,128)S(1)} all-to-all(f32[32,8,128]{2,1,0:T(8,128)S(1)} %bitcast.21), channel_id=1, replica_groups=mesh['ka'=16,'kp'=32] {'kp'}, dimensions={0} | all-to-all | bytes 262144 | tf_op jit(solution)/shard_map/all_to_all | solution.py:414
  78.2 3.1 %collective-permute-start = (f32[4,128]{1,0:T(4,128)S(1)}, f32[4,128]{1,0:T(4,128)S(1)}, u32[]{:S(2)}, u32[]{:S(2)}) collective-permute-start(f32[4,128]{1,0:T(4,128)S(1)} %get-tuple-element.16), channel_id=1, source_target_pairs={{12,0},{13,1},{14,32},{15,33},{8,64},{9,65},{10,96},{11,97},{20,12... | collective-permute-start | bytes 6152 | tf_op jit(solution)/shard_map/ppermute | solution.py:421
  81.3 0.1 reshape.72
  81.4 0.6 copy.14
  82.0 11.0 %collective-permute-done.block = f32[4,128]{1,0:T(4,128)S(1)} collective-permute-done((f32[4,128]{1,0:T(4,128)S(1)}, f32[4,128]{1,0:T(4,128)S(1)}, u32[]{:S(2)}, u32[]{:S(2)}) %collective-permute-start) | collective-permute-done | bytes 2080 | tf_op jit(solution)/shard_map/ppermute | solution.py:421
  93.0 0.7 last.1
  (20 shorter events, 0.2 us)
Async XLA Ops:
  0.6 45.8 %copy-start.6 = (f32[32,512]{1,0:T(8,128)S(1)}, f32[32,512]{1,0:T(8,128)}, u32[]{:S(2)}) copy-start(f32[32,512]{1,0:T(8,128)} %param.11) | copy-start | bytes 196612
  37.1 11.0 %copy-start.1 = (bf16[512,256]{1,0:T(8,128)(2,1)S(1)}, bf16[512,256]{1,0:T(8,128)(2,1)}, u32[]{:S(2)}) copy-start(bf16[512,256]{1,0:T(8,128)(2,1)} %constant.56.clone.edge) | copy-start | bytes 786436
  37.1 11.1 %copy-start.2 = (f32[2,128,128]{2,1,0:T(8,128)S(1)}, f32[2,128,128]{2,1,0:T(8,128)}, u32[]{:S(2)}) copy-start(f32[2,128,128]{2,1,0:T(8,128)} %constant.54.clone.base) | copy-start | bytes 393220
  37.1 11.1 %copy-start.4 = (f32[128,128]{1,0:T(8,128)S(1)}, f32[128,128]{1,0:T(8,128)}, u32[]{:S(2)}) copy-start(f32[128,128]{1,0:T(8,128)} %constant.55.clone.turns) | copy-start | bytes 196612
  39.4 19.7 %all-to-all-start.1 = ((bf16[416,4,128]{2,1,0:T(4,128)(2,1)}), bf16[416,4,128]{2,1,0:T(4,128)(2,1)S(1)}, u32[]{:S(2)}, u32[]{:S(2)}) async-start(bf16[416,4,128]{2,1,0:T(4,128)(2,1)} %second.1), calls=%async_computation.1 | async-start | bytes 851968 | tf_op jit(solution)/shard_map/all_to_all | solution.py:409
  48.2 10.9 %copy-start.3 = (bf16[2,128,128]{2,1,0:T(8,128)(2,1)S(1)}, bf16[2,128,128]{2,1,0:T(8,128)(2,1)}, u32[]{:S(2)}) copy-start(bf16[2,128,128]{2,1,0:T(8,128)(2,1)} %constant.57.clone.order) | copy-start | bytes 196612
  48.2 10.9 %copy-start.5 = (s32[2,1]{0,1:T(1,128)S(1)}, s32[2,1]{0,1:T(1,128)}, u32[]{:S(2)}) copy-start(s32[2,1]{0,1:T(1,128)} %param.12) | copy-start | bytes 28
  49.0 1.9 %copy-start = (bf16[16,512,256]{2,1,0:T(8,128)(2,1)}, bf16[16,512,256]{2,1,0:T(8,128)(2,1)S(1)}, u32[]{:S(2)}) copy-start(bf16[16,512,256]{2,1,0:T(8,128)(2,1)S(1)} %turns.1) | copy-start | bytes 12582916
  78.2 14.8 %collective-permute-start = (f32[4,128]{1,0:T(4,128)S(1)}, f32[4,128]{1,0:T(4,128)S(1)}, u32[]{:S(2)}, u32[]{:S(2)}) collective-permute-start(f32[4,128]{1,0:T(4,128)S(1)} %get-tuple-element.16), channel_id=1, source_target_pairs={{12,0},{13,1},{14,32},{15,33},{8,64},{9,65},{10,96},{11,97},{20,12... | collective-permute-start | bytes 6152 | tf_op jit(solution)/shard_map/ppermute | solution.py:421

commit v8 on v6

--- a/solution.py
+++ b/solution.py
@@ -137,8 +137,8 @@
             out[c, high : high + 128, 128:] = near[level]
 
 
-def second_kernel(place, slab, out):
-    own = slab[pl.ds(place[0] * SLAB, 8)]
+def second_kernel(slab, out):
+    own = slab[pl.ds(lax.axis_index("ka") * SLAB, 8)]
     lane = lax.broadcasted_iota(jnp.int32, (4, 128), 1)
     for i in range(out.shape[0] // BLOCK):
         half, start = i % 2, i // 2 * SLAB
@@ -381,7 +381,6 @@
     n_rows = lax.axis_size("ka")
     n_cols = lax.axis_size("kp")
     pair = pair_table.reshape(2)
-    place = lax.axis_index("ka").astype(jnp.int32).reshape(1)
 
     out = call_kernel(
         first_kernel,
@@ -401,16 +400,16 @@
         ],
     )
     slab = lax.all_to_all(out, "ka", 0, 0, tiled=True)
+    slab, plane_map, screen = lax.optimization_barrier((slab, plane_map, screen))
     out = call_kernel(
         second_kernel,
         "second",
-        place,
         slab,
-        scalars=1,
         outs=jax.ShapeDtypeStruct((n_cols * BLOCK, 4, 128), BF),
     )
     data = lax.all_to_all(out, "kp", 0, 0, tiled=True)
 
+    place = lax.axis_index("ka").astype(jnp.int32).reshape(1)
     screens = make_weight(screen, plane_map, plane_map.shape[0], OUTER * INNER)
     out = local_blocks(pair, place, data, slab, screens, make_turns())
 

time: 93.5 us -> 93.7 us (level)
  local copies, waits for them, and re-layouts: 2.93 us -> 5.59 us
  other arithmetic: 1.67 us -> 0.26 us
  waiting for transfers between devices: 37.4 us -> 36.3 us
    all_to_all x1, waiting for transfers between devices: 18.4 us -> 14.4 us  [shards(): slab = lax.all_to_all(out, 'ka', 0, 0, tiled=True)]
    all_to_all x1, waiting for transfers between devices: 8.08 us -> 10.9 us  [shards(): data = lax.all_to_all(out, 'kp', 0, 0, tiled=True)]
    unnamed x16 -> x18, local copies, waits for them, and re-layouts: 2.72 us -> 5.39 us
  transfers between devices with their start and end apart: 3 -> 3, of which waited for: 3 -> 3; matrix products, arithmetic and copies ran while one was open for 4% -> 3% of each run, Pallas kernels for 1% -> 1%
where the time goes in v8:
time: 93.7 us; the launch traced here: 93.2 us
  waiting for transfers between devices  36.3 us (39%)
  starting transfers between devices  26.1 us (28%)
  blocking collectives  12.2 us (13%)
  Pallas kernels  10.7 us (11%)
  local copies, waits for them, and re-layouts  5.59 us (6%)
  matrix products  1.24 us (1%)
    all_to_all x1, starting transfers between devices, shards(): slab = lax.all_to_all(out, 'ka', 0, 0, tiled=True)  15.9 us
    all_to_all x1, waiting for transfers between devices, shards(): slab = lax.all_to_all(out, 'ka', 0, 0, tiled=True)  14.4 us
    all_to_all x1, blocking collectives, shards(): parts = lax.all_to_all(out.reshape(n_cols, 8, 128), 'kp', 0, 0, tiled=True)  12.2 us
    ppermute x1, waiting for transfers between devices, shards(): adjoint = lax.ppermute(parts[:, 4:].sum(axis=0), ('ka', 'kp'), swap)  11 us
    all_to_all x1, waiting for transfers between devices, shards(): data = lax.all_to_all(out, 'kp', 0, 0, tiled=True)  10.9 us
    pallas_call x5, Pallas kernels, call_kernel(): call(body, out_shape=outs, in_specs=specs, out_specs=jax.tree.map(lambda...  10.7 us
    all_to_all x1, starting transfers between devices, shards(): data = lax.all_to_all(out, 'kp', 0, 0, tiled=True)  7.12 us
    unnamed x18, local copies, waits for them, and re-layouts  5.39 us
  transfers between devices with their start and end apart: 3, of which 3 were waited for; matrix products, arithmetic and copies ran while one was open for 3% of the time, Pallas kernels for 1%

profile of v8, /device:TPU:64, one launch (start us, length us, event | category | flops | bytes accessed | tf_op | source)
XLA Modules:
  0.0 93.2 jit_solution(13154289453001190289)
XLA Ops:
  0.6 1.5 %first.1 = bf16[176,4,128]{2,1,0:T(4,128)(2,1)} custom-call(s32[2]{0:T(128)} %bitcast.23, bf16[32,128]{1,0:T(8,128)(2,1)} %bitcast.27, bf16[8,64]{1,0:T(8,128)(2,1)} %bitcast.29, bf16[8,64]{1,0:T(8,128)(2,1)} %bitcast.30), custom_call_target="tpu_custom_call" | custom-call | tf_op jit(solution)/shard_map/first/pallas_call | solution.py:329
  2.1 15.9 %all-to-all-start = ((bf16[176,4,128]{2,1,0:T(4,128)(2,1)}), bf16[176,4,128]{2,1,0:T(4,128)(2,1)S(1)}, u32[]{:S(2)}, u32[]{:S(2)}) async-start(bf16[176,4,128]{2,1,0:T(4,128)(2,1)} %first.1), calls=%async_computation | async-start | bytes 360448 | tf_op jit(solution)/shard_map/all_to_all | solution.py:402
  18.0 0.0 copy-start.1
  18.0 0.9 %copy-done.1 = bf16[512,256]{1,0:T(8,128)(2,1)S(1)} copy-done((bf16[512,256]{1,0:T(8,128)(2,1)S(1)}, bf16[512,256]{1,0:T(8,128)(2,1)}, u32[]{:S(2)}) %copy-start.1) | copy-done | bytes 262168
  19.0 0.9 copy-done.2
  19.9 0.8 copy-done.4
  20.7 0.8 turns.2
  21.6 1.9 %copy-done = bf16[16,512,256]{2,1,0:T(8,128)(2,1)} copy-done((bf16[16,512,256]{2,1,0:T(8,128)(2,1)}, bf16[16,512,256]{2,1,0:T(8,128)(2,1)S(1)}, u32[]{:S(2)}) %copy-start) | copy-done | bytes 4194328
  23.5 14.4 %all-to-all-done.slab = bf16[176,4,128]{2,1,0:T(4,128)(2,1)S(1)} async-done(((bf16[176,4,128]{2,1,0:T(4,128)(2,1)}), bf16[176,4,128]{2,1,0:T(4,128)(2,1)S(1)}, u32[]{:S(2)}, u32[]{:S(2)}) %all-to-all-start) | async-done | bytes 180256 | tf_op jit(solution)/shard_map/all_to_all | solution.py:402
  37.9 0.9 second.1
  38.8 7.1 %all-to-all-start.1 = ((bf16[416,4,128]{2,1,0:T(4,128)(2,1)}), bf16[416,4,128]{2,1,0:T(4,128)(2,1)S(1)}, u32[]{:S(2)}, u32[]{:S(2)}) async-start(bf16[416,4,128]{2,1,0:T(4,128)(2,1)} %second.1), calls=%async_computation.1 | async-start | bytes 851968 | tf_op jit(solution)/shard_map/all_to_all | solution.py:410
  46.0 1.2 %fusion = f32[32,17,128]{2,0,1:T(8,128)S(1)} fusion(f32[32,1024]{1,0:T(8,128)S(1)} %pad_maximum_fusion, f32[17,1024]{1,0:T(8,128)S(1)} %add_convert_fusion, s32[1024]{0:T(1024)S(1)} %pad_add_fusion), kind=kOutput, calls=%fused_computation | convolution fusion | flops 856326144 | bytes 483328 | tf_op jit(solution)/shard_map/qcg,hg->qch/dot_general | solution.py:309
  47.3 0.1 slice.30
  47.4 0.1 pad_maximum_fusion.1
  47.5 0.1 copy.15
  47.7 0.1 maximum_maximum_fusion.screens
  47.7 10.9 %all-to-all-done.1.data = bf16[416,4,128]{2,1,0:T(4,128)(2,1)S(1)} async-done(((bf16[416,4,128]{2,1,0:T(4,128)(2,1)}), bf16[416,4,128]{2,1,0:T(4,128)(2,1)S(1)}, u32[]{:S(2)}, u32[]{:S(2)}) %all-to-all-start.1) | async-done | bytes 426016 | tf_op jit(solution)/shard_map/all_to_all | solution.py:410
  58.6 6.8 %pair_blocks.1 = f32[4,8,8,128]{3,2,1,0:T(8,128)S(1)} custom-call(s32[2]{0:T(128)S(1)} %bitcast.24, s32[1]{0:T(128)} %bitcast.1.place, bf16[416,4,128]{2,1,0:T(4,128)(2,1)S(1)} %all-to-all-done.1.data, bf16[176,4,128]{2,1,0:T(4,128)(2,1)S(1)} %all-to-all-done.slab, f32[32,16,256]{2,1,0:T(8,128)S(1)} %maximum_maximum_fusion.screens, ...), custom_call_target="tpu_custom_call" | custom-call | tf_op jit(solution)/shard_map/pair_blocks/pallas_call | solution.py:329
  65.5 12.2 %all_to_all.15 = f32[32,8,128]{2,1,0:T(8,128)S(1)} all-to-all(f32[32,8,128]{2,1,0:T(8,128)S(1)} %bitcast.22), channel_id=1, replica_groups=mesh['ka'=16,'kp'=32] {'kp'}, dimensions={0} | all-to-all | bytes 262144 | tf_op jit(solution)/shard_map/all_to_all | solution.py:416
  77.7 3.1 %collective-permute-start = (f32[4,128]{1,0:T(4,128)S(1)}, f32[4,128]{1,0:T(4,128)S(1)}, u32[]{:S(2)}, u32[]{:S(2)}) collective-permute-start(f32[4,128]{1,0:T(4,128)S(1)} %get-tuple-element.10), channel_id=1, source_target_pairs={{12,0},{13,1},{14,32},{15,33},{8,64},{9,65},{10,96},{11,97},{20,12... | collective-permute-start | bytes 6152 | tf_op jit(solution)/shard_map/ppermute | solution.py:423
  80.9 0.1 reshape.76
  81.0 0.6 copy.14
  81.5 11.0 %collective-permute-done.block = f32[4,128]{1,0:T(4,128)S(1)} collective-permute-done((f32[4,128]{1,0:T(4,128)S(1)}, f32[4,128]{1,0:T(4,128)S(1)}, u32[]{:S(2)}, u32[]{:S(2)}) %collective-permute-start) | collective-permute-done | bytes 2080 | tf_op jit(solution)/shard_map/ppermute | solution.py:423
  92.5 0.7 last.1
  (23 shorter events, 0.2 us)
Async XLA Ops:
  2.1 35.8 %all-to-all-start = ((bf16[176,4,128]{2,1,0:T(4,128)(2,1)}), bf16[176,4,128]{2,1,0:T(4,128)(2,1)S(1)}, u32[]{:S(2)}, u32[]{:S(2)}) async-start(bf16[176,4,128]{2,1,0:T(4,128)(2,1)} %first.1), calls=%async_computation | async-start | bytes 360448 | tf_op jit(solution)/shard_map/all_to_all | solution.py:402
  18.0 1.0 %copy-start.1 = (bf16[512,256]{1,0:T(8,128)(2,1)S(1)}, bf16[512,256]{1,0:T(8,128)(2,1)}, u32[]{:S(2)}) copy-start(bf16[512,256]{1,0:T(8,128)(2,1)} %constant.62.clone.edge) | copy-start | bytes 786436
  19.0 0.9 copy-start.2
  19.9 0.8 copy-start.4
  20.7 17.2 %copy-start.7 = (s32[512]{0:T(512)S(1)}, s32[512]{0:T(512)}, u32[]{:S(2)}) copy-start(s32[512]{0:T(512)} %param.13) | copy-start | bytes 6148
  20.7 25.3 %copy-start.6 = (f32[32,512]{1,0:T(8,128)S(1)}, f32[32,512]{1,0:T(8,128)}, u32[]{:S(2)}) copy-start(f32[32,512]{1,0:T(8,128)} %param.11) | copy-start | bytes 196612
  21.5 1.9 %copy-start = (bf16[16,512,256]{2,1,0:T(8,128)(2,1)}, bf16[16,512,256]{2,1,0:T(8,128)(2,1)S(1)}, u32[]{:S(2)}) copy-start(bf16[16,512,256]{2,1,0:T(8,128)(2,1)S(1)} %turns.2) | copy-start | bytes 12582916
  38.8 19.9 %copy-start.3 = (bf16[2,128,128]{2,1,0:T(8,128)(2,1)S(1)}, bf16[2,128,128]{2,1,0:T(8,128)(2,1)}, u32[]{:S(2)}) copy-start(bf16[2,128,128]{2,1,0:T(8,128)(2,1)} %constant.63.clone.order) | copy-start | bytes 196612
  38.8 19.9 %copy-start.5 = (s32[2,1]{0,1:T(1,128)S(1)}, s32[2,1]{0,1:T(1,128)}, u32[]{:S(2)}) copy-start(s32[2,1]{0,1:T(1,128)} %param.12) | copy-start | bytes 28
  38.8 19.8 %all-to-all-start.1 = ((bf16[416,4,128]{2,1,0:T(4,128)(2,1)}), bf16[416,4,128]{2,1,0:T(4,128)(2,1)S(1)}, u32[]{:S(2)}, u32[]{:S(2)}) async-start(bf16[416,4,128]{2,1,0:T(4,128)(2,1)} %second.1), calls=%async_computation.1 | async-start | bytes 851968 | tf_op jit(solution)/shard_map/all_to_all | solution.py:410
  77.7 14.8 %collective-permute-start = (f32[4,128]{1,0:T(4,128)S(1)}, f32[4,128]{1,0:T(4,128)S(1)}, u32[]{:S(2)}, u32[]{:S(2)}) collective-permute-start(f32[4,128]{1,0:T(4,128)S(1)} %get-tuple-element.10), channel_id=1, source_target_pairs={{12,0},{13,1},{14,32},{15,33},{8,64},{9,65},{10,96},{11,97},{20,12... | collective-permute-start | bytes 6152 | tf_op jit(solution)/shard_map/ppermute | solution.py:423
